TPU v7x, 256 devices: a whole 4x4x8 slice. The times are simulated.
256 devices in a mesh: img: 64 (over z, y, core), gy: 4 (over x).
Axes of the slice: x: 4, y: 4, z: 8, core: 2. Of those that a mesh axis runs over, the one named last changes fastest.
Arguments:
- path: float32 [256, 4, 128, 128], P('img', None, 'gy'), may hold values from -1.2 to 1.2
- start_image: float32 [4, 128, 128], P(None, 'gy'), may hold values from -1.2 to 1.2
- end_image: float32 [4, 128, 128], P(None, 'gy'), may hold values from -1.2 to 1.2
- labels: int32 [4, 128, 128], P(None, 'gy'), may hold values from 0 to 3
- mob_table: float32 [4], replicated, may hold values from 0.2 to 2
Outputs:
- new_path: float32 [256, 4, 128, 128], P('img', None, 'gy')
All inputs are finite; a program needn't handle non-finite values.
Results may differ from a plain program's by a relative error of at most 0.0001.
Values sent between devices are 32-bit elements; how exact they have to be, the bound alone decides.
A program may use at most 64 MiB of HBM per device.

v0:
```python
import functools

import jax
import jax.numpy as jnp
from jax import lax
from jax.sharding import Mesh
from jax.sharding import PartitionSpec as P

ITERS = 2
IMG = ("img_0", "img_1", "img_2")
IMG_GY = ("img_0", "img_1", "img_2", "gy")


time_step = 0.5
stiffness = 0.25
step_length = 0.05


def extended_2(shard, sides, width):
    for axis, dim in sides:
        size, length = (lax.axis_size(axis), shard.shape[dim])
        up = [(i, (i + 1) % size) for i in range(size - 1)]
        down = [(j, i) for i, j in up]
        last = lax.slice_in_dim(shard, length - width, length, axis=dim)
        initial = lax.slice_in_dim(shard, 0, width, axis=dim)
        before = lax.ppermute(last, axis, up)
        after = lax.ppermute(initial, axis, down)
        shard = jnp.concatenate([before, shard, after], axis=dim)
    return shard


def shifted(block, axis, distance):
    devices = range(lax.axis_size(axis))
    route = [(i - distance, i) for i in devices if i - distance in devices]
    return lax.ppermute(block, axis, route)


def by_axis(shard, axes):
    return functools.reduce(lax.psum, axes, shard)


def mobility(labels, table):
    result = jnp.zeros(labels.shape, jnp.float32)
    for level in range(table.shape[0]):
        result = result + jnp.where(labels == level, table[level], jnp.float32(0.0))
    return result


def laplace(padded):
    centre = padded[..., 1:-1, :]
    total = jnp.roll(centre, 1, -3) + jnp.roll(centre, -1, -3)
    total = total + jnp.roll(centre, 1, -1) + jnp.roll(centre, -1, -1)
    return total + padded[..., 2:, :] + padded[..., :-2, :] - 6.0 * centre


def drift(padded, mob):
    centre = padded[..., 1:-1, :]
    return mob * (stiffness * laplace(padded) + centre - centre * centre * centre)


def per_device(path, start_image, end_image, labels, mob_table):
    count = path.shape[0]
    groups = lax.axis_size(IMG)
    images = count * groups
    rank = lax.axis_index(IMG)
    is_first = rank == 0
    is_final = rank == groups - 1
    gy_rank = lax.axis_index("gy")
    gy_count = lax.axis_size("gy")
    rows_here = path.shape[2]
    cells = images * path.shape[1] * rows_here * gy_count * path.shape[3]
    labels_wide = extended_2(labels, (("gy", 1),), 1)
    mob_wide = mobility(labels_wide, mob_table)
    rows = jnp.arange(rows_here + 2)
    outside = (rows == 0) & (gy_rank == 0) | (rows == rows_here + 1) & (gy_rank == gy_count - 1)
    inside = jnp.where(outside, jnp.float32(0.0), jnp.float32(1.0))[:, None]
    for step in range(ITERS):
        extended = jnp.concatenate([start_image[None], path, end_image[None]], 0)
        padded = extended_2(extended, (("gy", 2),), 2)
        finish = padded[count + 1, :, 1:-1, :]
        force = drift(padded[: count + 1], mob_wide)
        current = padded[1 : count + 1, :, 1:-1, :]
        start_part = padded[0, :, 1:-1, :]
        ahead = shifted(current[0], IMG, -1)
        ahead = jnp.where(is_final, finish, ahead)
        later = jnp.concatenate([current[1:], ahead[None]], 0)
        wide_res = (later - current) / time_step - force[1:]
        opening = (current[0] - start_part) / time_step - force[0]
        resid = wide_res[:, :, 1:-1, :]
        opening_in = opening[:, 1:-1, :]
        mpad = mob_wide * wide_res * inside
        mres = mpad[:, :, 1:-1, :]
        previous = shifted(resid[-1], IMG, 1)
        previous = jnp.where(is_first, opening_in, previous)
        earlier = jnp.concatenate([previous[None], resid[:-1]], 0)
        adjoint = stiffness * laplace(mpad) + (1.0 - 3.0 * path * path) * mres
        grad = (earlier - resid) / time_step - adjoint
        flat = grad.reshape(count, groups, -1)
        columns = lax.all_to_all(flat, IMG, split_axis=1, concat_axis=0, tiled=True)
        every = columns.shape[0]
        index = jnp.arange(1, every + 1).astype(jnp.float32)[:, None, None]
        scaled = index * columns
        before_g = jnp.cumsum(columns, 0) - columns
        before_q = jnp.cumsum(scaled, 0) - scaled
        coeff = jnp.sum(columns, 0) - jnp.sum(scaled, 0) / (every + 1)
        solved = time_step * time_step * (index * coeff[None] - index * before_g + before_q)
        back = lax.all_to_all(solved, IMG, split_axis=0, concat_axis=1, tiled=True)
        update = back.reshape(grad.shape)
        squares = by_axis(jnp.sum(update * update), IMG_GY)
        scale = step_length * lax.rsqrt(squares / cells + 1e-06)
        path = path - scale * update
    return path


def solution(mesh):
    split = Mesh(mesh.devices.reshape(8, 4, 2, mesh.shape["gy"]), ("img_0", "img_1", "img_2", "gy"))
    placed = (
        P(IMG, None, "gy", None),
        P(None, "gy", None),
        P(None, "gy", None),
        P(None, "gy", None),
        P(),
    )
    return jax.shard_map(
        per_device, mesh=split, in_specs=placed, out_specs=P(IMG, None, "gy", None), check_vma=False
    )
```

profile of v0, /device:TPU:1, one launch (start us, length us, event | category | flops | bytes accessed | tf_op | source)
XLA Modules:
  0.0 220.0 jit_solution(11074976946567192362)
XLA Ops:
  0.0 0.7 fusion.92
  0.7 1.3 collective-permute-start.3
  2.0 4.6 %collective-permute-start.2 = (s32[4,1,128]{2,1,0:T(1,128)S(1)}, s32[4,1,128]{2,1,0:T(1,128)S(1)}, u32[]{:S(2)}, u32[]{:S(2)}) collective-permute-start(s32[4,1,128]{2,1,0:T(1,128)S(1)} %get-tuple-element.53), channel_id=1, source_target_pairs={{0,1},{1,2},{2,3},{4,5},{5,6},{6,7},{8,9},{9,10},{10,11},{12,13},{... | collective-permute-start | bytes 6152 | tf_op jit(solution)/shard_map/ppermute | solution.py:26
  6.7 1.1 pad_maximum_fusion.13
  7.8 3.5 %collective-permute-start = (f32[6,4,2,128]{3,2,1,0:T(2,128)S(1)}, f32[6,4,2,128]{3,2,1,0:T(2,128)S(1)}, u32[]{:S(2)}, u32[]{:S(2)}) collective-permute-start(f32[6,4,2,128]{3,2,1,0:T(2,128)S(1)} %get-tuple-element.36), channel_id=1, source_target_pairs={{0,1},{1,2},{2,3},{4,5},{5,6},{6,7},{8,9},{9,10},{10,11},{12,13},{... | collective-permute-start | bytes 73736 | tf_op jit(solution)/shard_map/ppermute | solution.py:26
  11.3 1.3 collective-permute-start.1
  12.6 0.7 fusion.93
  13.3 2.6 %select_add_fusion = f32[4,34,128]{2,1,0:T(8,128)S(1)} fusion(s32[4,1,128]{2,1,0:T(1,128)S(1)} %collective-permute-done.3, s32[4,32,128]{2,1,0:T(8,128)S(1)} %copy-done.3, s32[4,1,128]{2,1,0:T(1,128)S(1)} %collective-permute-done.2, f32[]{:T(128)} %bitcast.7, f32[]{:T(128)} %bitcast.6, f32[]{:T(128)} %bitcast.5, f32[]{:T(128)} %bitcast.4), kind=kLoop, calls=%fused_computation.125 | loop fusion | flops 226304 | bytes 139280 | tf_op jit(solution)/shard_map/add | solution.py:45
  16.1 0.2 fusion.78
  16.3 0.2 fusion.79
  16.5 4.8 %collective-permute-start.4 = (f32[4,34,128]{2,1,0:T(8,128)S(1)}, f32[4,34,128]{2,1,0:T(8,128)S(1)}, u32[]{:S(2)}, u32[]{:S(2)}) collective-permute-start(f32[4,34,128]{2,1,0:T(8,128)S(1)} %get-tuple-element.24), channel_id=1, source_target_pairs={{4,0},{8,4},{12,8},{16,12},{20,16},{24,20},{28,24},{32,28},{36,32}... | collective-permute-start | bytes 208904 | tf_op jit(solution)/shard_map/ppermute | solution.py:35
  21.2 0.5 fusion.11
  21.8 2.5 %collective-permute-done.4 = f32[4,34,128]{2,1,0:T(8,128)S(1)} collective-permute-done((f32[4,34,128]{2,1,0:T(8,128)S(1)}, f32[4,34,128]{2,1,0:T(8,128)S(1)}, u32[]{:S(2)}, u32[]{:S(2)}) %collective-permute-start.4) | collective-permute-done | bytes 69664 | tf_op jit(solution)/shard_map/ppermute | solution.py:35
  24.5 0.1 fusion.88
  24.6 0.1 fusion.89
  24.8 1.9 collective-permute-start.5
  26.7 1.3 collective-permute-done.5
  28.0 0.4 fusion.31
  28.5 0.9 copy.20
  29.3 13.6 %all-to-all-start = ((f32[4,64,256]{2,0,1:T(4,128)}), f32[4,64,256]{2,0,1:T(4,128)S(1)}, u32[]{:S(2)}, u32[]{:S(2)}) async-start(f32[4,64,256]{2,0,1:T(4,128)} %copy.20), calls=%async_computation | async-start | bytes 524288 | tf_op jit(solution)/shard_map/all_to_all | solution.py:99
  42.9 13.2 %all-to-all-done = f32[4,64,256]{2,0,1:T(4,128)S(1)} async-done(((f32[4,64,256]{2,0,1:T(4,128)}), f32[4,64,256]{2,0,1:T(4,128)S(1)}, u32[]{:S(2)}, u32[]{:S(2)}) %all-to-all-start) | async-done | bytes 262176 | tf_op jit(solution)/shard_map/all_to_all | solution.py:99
  56.1 0.2 all_to_all.41
  56.3 0.4 fusion.73
  56.7 0.2 fusion.58
  56.9 0.2 fusion.60
  57.3 0.3 reshape.451
  57.6 0.3 reshape.446
  58.0 1.8 fusion.51
  59.8 17.7 %all_to_all.54 = f32[256,1,256]{2,1,0:T(1,128)S(1)} all-to-all(f32[256,1,256]{2,1,0:T(1,128)S(1)} %fusion.51), channel_id=1, replica_groups=mesh['img_0'=8,'img_1'=4,'img_2'=2,'gy'=4] {'img_0','img_1','img_2'}, dimensions={0} | all-to-all | bytes 524288 | tf_op jit(solution)/shard_map/all_to_all | solution.py:107
  77.5 1.1 multiply_reduce_fusion.1
  78.6 12.2 %psum.56 = f32[]{:T(128)} all-reduce(f32[]{:T(128)} %multiply_reduce_fusion.1), channel_id=1, replica_groups=mesh['img_0'=8,'img_1'=4,'img_2'=2,'gy'=4] {'img_0'}, use_global_device_ids=true, to_apply=%region_7.8 | all-reduce | flops 1 | bytes 8 | tf_op jit(solution)/shard_map/psum | solution.py:39
  90.8 7.3 %psum.57 = f32[]{:T(128)} all-reduce(f32[]{:T(128)} %psum.56), channel_id=1, replica_groups=mesh['img_0'=8,'img_1'=4,'img_2'=2,'gy'=4] {'img_1'}, use_global_device_ids=true, to_apply=%region_8.9 | all-reduce | flops 1 | bytes 8 | tf_op jit(solution)/shard_map/psum | solution.py:39
  98.1 9.4 %psum.58 = f32[]{:T(128)} all-reduce(f32[]{:T(128)} %psum.57), channel_id=1, replica_groups=mesh['img_0'=8,'img_1'=4,'img_2'=2,'gy'=4] {'img_2'}, use_global_device_ids=true, to_apply=%region_9.10 | all-reduce | flops 1 | bytes 8 | tf_op jit(solution)/shard_map/psum | solution.py:39
  107.5 9.0 %psum.59 = f32[]{:T(128)} all-reduce(f32[]{:T(128)} %psum.58), channel_id=1, replica_groups=mesh['img_0'=8,'img_1'=4,'img_2'=2,'gy'=4] {'gy'}, use_global_device_ids=true, to_apply=%region_10.11 | all-reduce | flops 1 | bytes 8 | tf_op jit(solution)/shard_map/psum | solution.py:39
  117.4 2.1 collective-permute-start.6
  119.6 1.3 collective-permute-start.7
  120.9 3.3 %collective-permute-done.7 = f32[6,4,2,128]{3,2,1,0:T(2,128)S(1)} collective-permute-done((f32[6,4,2,128]{3,2,1,0:T(2,128)S(1)}, f32[6,4,2,128]{3,2,1,0:T(2,128)S(1)}, u32[]{:S(2)}, u32[]{:S(2)}) %collective-permute-start.7) | collective-permute-done | bytes 24608 | tf_op jit(solution)/shard_map/ppermute | solution.py:27
  124.3 0.2 fusion.74
  124.5 0.2 fusion.75
  124.7 5.7 %collective-permute-start.8 = (f32[4,34,128]{2,1,0:T(8,128)S(1)}, f32[4,34,128]{2,1,0:T(8,128)S(1)}, u32[]{:S(2)}, u32[]{:S(2)}) collective-permute-start(f32[4,34,128]{2,1,0:T(8,128)S(1)} %get-tuple-element.14), channel_id=1, source_target_pairs={{4,0},{8,4},{12,8},{16,12},{20,16},{24,20},{28,24},{32,28},{36,32}... | collective-permute-start | bytes 208904 | tf_op jit(solution)/shard_map/ppermute | solution.py:35
  130.4 0.5 fusion.19
  130.9 1.5 collective-permute-done.8
  132.5 0.1 multiply_multiply_fusion.4
  132.6 0.1 fusion.84
  132.8 0.1 fusion.85
  132.9 1.9 collective-permute-start.9
  134.9 1.3 collective-permute-done.9
  136.2 0.4 fusion.35
  136.6 0.2 copy.28
  136.8 23.6 %all_to_all.55 = f32[4,64,256]{2,0,1:T(4,128)S(1)} all-to-all(f32[4,64,256]{2,0,1:T(4,128)S(1)} %copy.28), channel_id=1, replica_groups=mesh['img_0'=8,'img_1'=4,'img_2'=2,'gy'=4] {'img_0','img_1','img_2'}, dimensions={1} | all-to-all | bytes 524288 | tf_op jit(solution)/shard_map/all_to_all | solution.py:99
  160.4 0.2 all_to_all.46
  160.6 0.4 fusion.72
  161.0 0.2 fusion.54
  161.3 0.2 fusion.56
  161.6 0.3 reshape.462
  161.9 0.3 reshape.457
  162.3 1.8 fusion.47
  164.2 17.7 %all_to_all.56 = f32[256,1,256]{2,1,0:T(1,128)S(1)} all-to-all(f32[256,1,256]{2,1,0:T(1,128)S(1)} %fusion.47), channel_id=1, replica_groups=mesh['img_0'=8,'img_1'=4,'img_2'=2,'gy'=4] {'img_0','img_1','img_2'}, dimensions={0} | all-to-all | bytes 524288 | tf_op jit(solution)/shard_map/all_to_all | solution.py:107
  181.8 1.1 multiply_reduce_fusion
  183.0 12.2 %psum.60 = f32[]{:T(128)} all-reduce(f32[]{:T(128)} %multiply_reduce_fusion), channel_id=1, replica_groups=mesh['img_0'=8,'img_1'=4,'img_2'=2,'gy'=4] {'img_0'}, use_global_device_ids=true, to_apply=%region_18.19 | all-reduce | flops 1 | bytes 8 | tf_op jit(solution)/shard_map/psum | solution.py:39
  195.1 7.3 %psum.61 = f32[]{:T(128)} all-reduce(f32[]{:T(128)} %psum.60), channel_id=1, replica_groups=mesh['img_0'=8,'img_1'=4,'img_2'=2,'gy'=4] {'img_1'}, use_global_device_ids=true, to_apply=%region_19.20 | all-reduce | flops 1 | bytes 8 | tf_op jit(solution)/shard_map/psum | solution.py:39
  202.4 9.4 %psum.62 = f32[]{:T(128)} all-reduce(f32[]{:T(128)} %psum.61), channel_id=1, replica_groups=mesh['img_0'=8,'img_1'=4,'img_2'=2,'gy'=4] {'img_2'}, use_global_device_ids=true, to_apply=%region_20.21 | all-reduce | flops 1 | bytes 8 | tf_op jit(solution)/shard_map/psum | solution.py:39
  211.8 6.7 %psum.63 = f32[]{:T(128)} all-reduce(f32[]{:T(128)} %psum.62), channel_id=1, replica_groups=mesh['img_0'=8,'img_1'=4,'img_2'=2,'gy'=4] {'gy'}, use_global_device_ids=true, to_apply=%region_21.22 | all-reduce | flops 1 | bytes 8 | tf_op jit(solution)/shard_map/psum | solution.py:39
  219.3 0.7 sub.131
  (82 shorter events, 1.8 us)
Async XLA Ops:
  0.7 12.6 %collective-permute-start.3 = (s32[4,1,128]{2,1,0:T(1,128)S(1)}, s32[4,1,128]{2,1,0:T(1,128)S(1)}, u32[]{:S(2)}, u32[]{:S(2)}) collective-permute-start(s32[4,1,128]{2,1,0:T(1,128)S(1)} %get-tuple-element.54), channel_id=1, source_target_pairs={{1,0},{2,1},{3,2},{5,4},{6,5},{7,6},{9,8},{10,9},{11,10},{13,12},{... | collective-permute-start | bytes 6152 | tf_op jit(solution)/shard_map/ppermute | solution.py:27
  2.0 11.3 %collective-permute-start.2 = (s32[4,1,128]{2,1,0:T(1,128)S(1)}, s32[4,1,128]{2,1,0:T(1,128)S(1)}, u32[]{:S(2)}, u32[]{:S(2)}) collective-permute-start(s32[4,1,128]{2,1,0:T(1,128)S(1)} %get-tuple-element.53), channel_id=1, source_target_pairs={{0,1},{1,2},{2,3},{4,5},{5,6},{6,7},{8,9},{9,10},{10,11},{12,13},{... | collective-permute-start | bytes 6152 | tf_op jit(solution)/shard_map/ppermute | solution.py:26
  6.6 6.0 %copy-start.4 = (f32[4]{0:T(128)S(1)}, f32[4]{0:T(128)}, u32[]{:S(2)}) copy-start(f32[4]{0:T(128)} %param.9) | copy-start | bytes 52
  6.6 6.7 %copy-start.3 = (s32[4,32,128]{2,1,0:T(8,128)S(1)}, s32[4,32,128]{2,1,0:T(8,128)}, u32[]{:S(2)}) copy-start(s32[4,32,128]{2,1,0:T(8,128)} %param.8) | copy-start | bytes 196612
  6.6 9.3 %copy-start.1 = (f32[4,32,128]{2,1,0:T(8,128)S(1)}, f32[4,32,128]{2,1,0:T(8,128)}, u32[]{:S(2)}) copy-start(f32[4,32,128]{2,1,0:T(8,128)} %param.7) | copy-start | bytes 196612
  6.6 9.3 %copy-start.2 = (f32[4,32,128]{2,1,0:T(8,128)S(1)}, f32[4,32,128]{2,1,0:T(8,128)}, u32[]{:S(2)}) copy-start(f32[4,32,128]{2,1,0:T(8,128)} %param.6) | copy-start | bytes 196612
  7.8 8.2 %copy-start = (f32[4,4,32,128]{3,2,1,0:T(8,128)S(1)}, f32[4,4,32,128]{3,2,1,0:T(8,128)}, u32[]{:S(2)}) copy-start(f32[4,4,32,128]{3,2,1,0:T(8,128)} %param.5) | copy-start | bytes 786436
  7.8 8.1 %collective-permute-start = (f32[6,4,2,128]{3,2,1,0:T(2,128)S(1)}, f32[6,4,2,128]{3,2,1,0:T(2,128)S(1)}, u32[]{:S(2)}, u32[]{:S(2)}) collective-permute-start(f32[6,4,2,128]{3,2,1,0:T(2,128)S(1)} %get-tuple-element.36), channel_id=1, source_target_pairs={{0,1},{1,2},{2,3},{4,5},{5,6},{6,7},{8,9},{9,10},{10,11},{12,13},{... | collective-permute-start | bytes 73736 | tf_op jit(solution)/shard_map/ppermute | solution.py:26
  11.3 4.6 %collective-permute-start.1 = (f32[6,4,2,128]{3,2,1,0:T(2,128)S(1)}, f32[6,4,2,128]{3,2,1,0:T(2,128)S(1)}, u32[]{:S(2)}, u32[]{:S(2)}) collective-permute-start(f32[6,4,2,128]{3,2,1,0:T(2,128)S(1)} %get-tuple-element.35), channel_id=1, source_target_pairs={{1,0},{2,1},{3,2},{5,4},{6,5},{7,6},{9,8},{10,9},{11,10},{13,12},{... | collective-permute-start | bytes 73736 | tf_op jit(solution)/shard_map/ppermute | solution.py:27
  16.5 7.8 %collective-permute-start.4 = (f32[4,34,128]{2,1,0:T(8,128)S(1)}, f32[4,34,128]{2,1,0:T(8,128)S(1)}, u32[]{:S(2)}, u32[]{:S(2)}) collective-permute-start(f32[4,34,128]{2,1,0:T(8,128)S(1)} %get-tuple-element.24), channel_id=1, source_target_pairs={{4,0},{8,4},{12,8},{16,12},{20,16},{24,20},{28,24},{32,28},{36,32}... | collective-permute-start | bytes 208904 | tf_op jit(solution)/shard_map/ppermute | solution.py:35
  24.8 3.2 %collective-permute-start.5 = (f32[4,32,128]{2,1,0:T(8,128)S(1)}, f32[4,32,128]{2,1,0:T(8,128)S(1)}, u32[]{:S(2)}, u32[]{:S(2)}) collective-permute-start(f32[4,32,128]{2,1,0:T(8,128)S(1)} %slice_bitcast_fusion.9), channel_id=1, source_target_pairs={{0,4},{4,8},{8,12},{12,16},{16,20},{20,24},{24,28},{28,32},{32,36}... | collective-permute-start | bytes 196616 | tf_op jit(solution)/shard_map/ppermute | solution.py:35
  29.3 26.7 %all-to-all-start = ((f32[4,64,256]{2,0,1:T(4,128)}), f32[4,64,256]{2,0,1:T(4,128)S(1)}, u32[]{:S(2)}, u32[]{:S(2)}) async-start(f32[4,64,256]{2,0,1:T(4,128)} %copy.20), calls=%async_computation | async-start | bytes 524288 | tf_op jit(solution)/shard_map/all_to_all | solution.py:99
  117.4 3.5 %collective-permute-start.6 = (f32[6,4,2,128]{3,2,1,0:T(2,128)S(1)}, f32[6,4,2,128]{3,2,1,0:T(2,128)S(1)}, u32[]{:S(2)}, u32[]{:S(2)}) collective-permute-start(f32[6,4,2,128]{3,2,1,0:T(2,128)S(1)} %get-tuple-element.34), channel_id=1, source_target_pairs={{0,1},{1,2},{2,3},{4,5},{5,6},{6,7},{8,9},{9,10},{10,11},{12,13},{... | collective-permute-start | bytes 73736 | tf_op jit(solution)/shard_map/ppermute | solution.py:26
  119.6 4.6 %collective-permute-start.7 = (f32[6,4,2,128]{3,2,1,0:T(2,128)S(1)}, f32[6,4,2,128]{3,2,1,0:T(2,128)S(1)}, u32[]{:S(2)}, u32[]{:S(2)}) collective-permute-start(f32[6,4,2,128]{3,2,1,0:T(2,128)S(1)} %get-tuple-element.33), channel_id=1, source_target_pairs={{1,0},{2,1},{3,2},{5,4},{6,5},{7,6},{9,8},{10,9},{11,10},{13,12},{... | collective-permute-start | bytes 73736 | tf_op jit(solution)/shard_map/ppermute | solution.py:27
  124.7 7.8 %collective-permute-start.8 = (f32[4,34,128]{2,1,0:T(8,128)S(1)}, f32[4,34,128]{2,1,0:T(8,128)S(1)}, u32[]{:S(2)}, u32[]{:S(2)}) collective-permute-start(f32[4,34,128]{2,1,0:T(8,128)S(1)} %get-tuple-element.14), channel_id=1, source_target_pairs={{4,0},{8,4},{12,8},{16,12},{20,16},{24,20},{28,24},{32,28},{36,32}... | collective-permute-start | bytes 208904 | tf_op jit(solution)/shard_map/ppermute | solution.py:35
  132.9 3.2 %collective-permute-start.9 = (f32[4,32,128]{2,1,0:T(8,128)S(1)}, f32[4,32,128]{2,1,0:T(8,128)S(1)}, u32[]{:S(2)}, u32[]{:S(2)}) collective-permute-start(f32[4,32,128]{2,1,0:T(8,128)S(1)} %slice_bitcast_fusion.8), channel_id=1, source_target_pairs={{0,4},{4,8},{8,12},{12,16},{16,20},{20,24},{24,28},{28,32},{32,36}... | collective-permute-start | bytes 196616 | tf_op jit(solution)/shard_map/ppermute | solution.py:35
where the time goes:
time: 222 us; the launch traced here: 220 us
  blocking collectives  132 us (59%)
  starting transfers between devices  42 us (19%)
  waiting for transfers between devices  23 us (10%)
  other arithmetic  14.5 us (7%)
  local copies, waits for them, and re-layouts  6.13 us (3%)
    psum x8, blocking collectives, by_axis(): return functools.reduce(lax.psum, axes, shard)  73.4 us
    all_to_all x2, blocking collectives, per_device(): back = lax.all_to_all(solved, IMG, split_axis=0, concat_axis=1, tiled=True)  35.3 us
    all_to_all x1, blocking collectives, per_device(): columns = lax.all_to_all(flat, IMG, split_axis=1, concat_axis=0, tiled=True)  23.6 us
    ppermute x4, starting transfers between devices, shifted(): return lax.ppermute(block, axis, route)  14.3 us
    all_to_all x1, starting transfers between devices, per_device(): columns = lax.all_to_all(flat, IMG, split_axis=1, concat_axis=0, tiled=True)  13.6 us
    all_to_all x1, waiting for transfers between devices, per_device(): columns = lax.all_to_all(flat, IMG, split_axis=1, concat_axis=0, tiled=True)  13.2 us
    ppermute x3, starting transfers between devices, extended_2(): before = lax.ppermute(last, axis, up)  10.2 us
    ppermute x4, waiting for transfers between devices, shifted(): return lax.ppermute(block, axis, route)  6.59 us
  transfers between devices with their start and end apart: 11, of which 6 were waited for; matrix products, arithmetic and copies ran while one was open for 2% of the time, Pallas kernels for 0%

commit v1 on v0

v1 whole, which is shorter than its diff:
```python
import jax
import jax.numpy as jnp
from jax import lax
from jax.experimental import pallas as pl
from jax.experimental.pallas import tpu as pltpu
from jax.sharding import PartitionSpec as P

ITERS = 2
NZ, NK, NX = 8, 8, 4
G = 4
stiffness = 0.25
step_length = 0.05
MESH = pl.DeviceIdType.MESH


def ring(n, d):
    return min(d % n, -d % n)


PLANE = sorted(
    [(dy, dc) for dy in range(4) for dc in range(2) if dy or dc], key=lambda o: (-ring(4, o[0]), -o[1])
)
ZS = sorted(range(1, NZ), key=lambda d: -ring(NZ, d))
NEAR = sorted(
    [(dy, dc, dx) for dy in range(4) for dc in range(2) for dx in range(NX) if dy or dc or dx],
    key=lambda o: (-ring(4, o[0]) - ring(4, o[2]), -o[1]),
)


def laplace(v, sub):
    total = jnp.concatenate([v[1:], v[:1]], 0) + jnp.concatenate([v[-1:], v[:-1]], 0)
    total = total + pltpu.roll(v, 1, 3) + pltpu.roll(v, 127, 3)
    up = pltpu.roll(v, 7, 2)
    total = total + jnp.where(sub == 7, jnp.concatenate([up[:, 1:], up[:, :1]], 1), up)
    down = pltpu.roll(v, 1, 2)
    total = total + jnp.where(sub == 0, jnp.concatenate([down[:, -1:], down[:, :-1]], 1), down)
    return total - 6.0 * v


def kernel(
    path, start, end, labels, table, out,
    own, lab, edge, nxt, prv, labx, state, vbuf, mobb,
    s1, r1, ef, s2, r2, sr, rr, ud, s3, r3, r3h, sa, ra,
    loc, init_s, init_r, snd, rcv,
):
    img, gy = lax.axis_index("img"), lax.axis_index("gy")
    z, k = img // NK, img % NK
    y, c = k // 2, k % 2
    n_img = NZ * NK
    right, left = (img + 1) % n_img, (img + n_img - 1) % n_img
    above, below = (gy + 1) % NX, (gy + NX - 1) % NX

    def member(dy, dc):
        return ((y + dy) % 4) * 2 + (c + dc) % 2

    local = [
        pltpu.make_async_copy(path, own.at[pl.ds(0, G)], loc.at[0]),
        pltpu.make_async_copy(start, own.at[G], loc.at[1]),
        pltpu.make_async_copy(end, own.at[G + 1], loc.at[2]),
        pltpu.make_async_copy(labels, lab, loc.at[3]),
    ]
    for copy in local:
        copy.start()

    barrier = pltpu.get_barrier_semaphore()

    def greet(i, x):
        pl.semaphore_signal(barrier, inc=1, device_id=(i, x), device_id_type=MESH)

    for d in ZS:
        greet(((z + d) % NZ) * NK + k, gy)
    for dy, dc, dx in NEAR:
        greet(z * NK + member(dy, dc), (gy + dx) % NX)

    @pl.when(k == 0)
    def _():
        for x in (gy, above, below):
            greet(left, x)

    @pl.when(k == NK - 1)
    def _():
        for x in (gy, above, below):
            greet(right, x)

    at_end = jnp.where((k == 0) | (k == NK - 1), 3, 0)
    for copy in local:
        copy.wait()
    pl.semaphore_wait(barrier, len(ZS) + len(NEAR) + at_end)

    to_right = jnp.where(img == n_img - 1, G, G - 1)
    to_left = jnp.where(img == 0, G + 1, 0)
    moves = [
        (own.at[to_right], edge.at[0], right, gy),
        (own.at[to_left], edge.at[1], left, gy),
        (own.at[to_right, :, 3], prv.at[0], right, above),
        (own.at[to_right, :, 0], nxt.at[0], right, below),
        (own.at[to_left, :, 3], prv.at[G + 1], left, above),
        (own.at[to_left, :, 0], nxt.at[G + 1], left, below),
        (lab.at[:, 3], labx.at[0], img, above),
        (lab.at[:, 0], labx.at[1], img, below),
        (own.at[pl.ds(0, G), :, 3], prv.at[pl.ds(1, G)], img, above),
        (own.at[pl.ds(0, G), :, 0], nxt.at[pl.ds(1, G)], img, below),
    ]
    halo = [
        pltpu.make_async_remote_copy(a, b, init_s.at[n], init_r.at[n], device_id=(i, x), device_id_type=MESH)
        for n, (a, b, i, x) in enumerate(moves)
    ]
    for copy in halo:
        copy.start()
    for copy in halo:
        copy.wait_recv()

    shape = (4, 5, 8, 128)
    sub = lax.broadcasted_iota(jnp.int32, shape, 2)
    low = lax.broadcasted_iota(jnp.int32, (4, 1, 8, 128), 2) < 4
    has_next = jnp.where(gy < NX - 1, jnp.float32(1.0), jnp.float32(0.0))
    has_prev = jnp.where(gy > 0, jnp.float32(1.0), jnp.float32(0.0))
    inside = jnp.where(low, has_next, has_prev)

    every = jnp.concatenate([lab[...], jnp.where(low, labx[1][:, None], labx[0][:, None])], 1)
    mob = jnp.zeros(shape, jnp.float32)
    for level in range(4):
        mob = jnp.where(every == level, table[level], mob)
    mobb[...] = jnp.concatenate([mob[:, :4], mob[:, 4:] * inside], 1)

    for i in range(G + 2):
        centre = edge[0] if i == 0 else edge[1] if i == G + 1 else own[i - 1]
        side = jnp.where(low, nxt[i][:, None], prv[i][:, None]) * inside
        state[i] = jnp.concatenate([centre, side], 1)

    def send(src, dst, it, n, i, x):
        copy = pltpu.make_async_remote_copy(
            src, dst, snd.at[it, n], rcv.at[it, n], device_id=(i, x), device_id_type=MESH
        )
        copy.start()

    def bytes_of(ref, sem):
        pltpu.make_async_copy(ref, ref, sem).wait()

    cells = n_img * G * 4 * 32 * NX * 128
    for it in range(ITERS):
        mob = mobb[...]
        before = None
        hs = []
        for i in range(G + 1):
            p = state[i]
            force = mob * (stiffness * laplace(p, sub) + p - p * p * p)
            r = (state[i + 1] - p) * 2.0 - force
            if i:
                m = mob * r
                adjoint = stiffness * laplace(m, sub) + (1.0 - 3.0 * p * p) * m
                hs.append(0.25 * ((before - r) * 2.0 - adjoint))
            before = r
        h1, h2, h3, h4 = hs
        v2 = -h1
        v3 = 2.0 * v2 - h2
        v4 = 2.0 * v3 - v2 - h3
        v5 = 2.0 * v4 - v3 - h4
        for n, v in enumerate((v2, v3, v4, v5)):
            vbuf[n] = v
        sums = (
            h1 + h2 + h3 + h4,
            h1 + 2.0 * h2 + 3.0 * h3 + 4.0 * h4,
            v2 + v3 + v4,
            2.0 * v2 + 3.0 * v3 + 4.0 * v4,
        )
        squares = (v2 * v2 + v3 * v3 + v4 * v4)[:, :4]
        squares = jnp.sum(jnp.sum(squares, 0), 0)
        for n, v in enumerate(sums):
            for share in range(NK):
                t = (share % 2) * 2
                s1[it, share, n] = v[share // 2, t : t + 2]
        for dy, dc in PLANE:
            other = member(dy, dc)
            send(s1.at[it, other], r1.at[it, k], it, 0, z * NK + other, gy)
        r1[it, k] = s1[it, k]
        bytes_of(r1.at[it, pl.ds(0, NK - 1)], rcv.at[it, 0])
        before_p = jnp.zeros((2, 8, 128), jnp.float32)
        before_q = before_p
        y0, y1, y2 = before_p, before_p, before_p
        for n in range(NK):
            p, q, w0, w1 = (r1[it, n, m] for m in range(4))
            f = -before_p
            e = before_q - (4.0 * n) * before_p
            ef[n, 0], ef[n, 1] = e, f
            y0 = y0 + 4.0 * e + 10.0 * f + w0
            y1 = y1 + (16.0 * n + 10.0) * e + (40.0 * n + 30.0) * f + (4.0 * n) * w0 + w1
            y2 = y2 + e * (4.0 * e + 20.0 * f + 2.0 * w0) + f * (30.0 * f + 2.0 * w1)
            before_q = before_q + (4.0 * n) * p + q
            before_p = before_p + p
        first = (z * (G * NK)).astype(jnp.float32)
        for n, v in enumerate((before_p, before_q + first * before_p, y0, y1)):
            s2[it, n] = v
            r2[it, z, n] = v
        row = jnp.sum(y2[0] + y2[1] + squares, 0, keepdims=True)
        sr[it] = row
        rr[it, z] = row
        for d in ZS:
            other = (z + d) % NZ
            send(s2.at[it], r2.at[it, z], it, 1, other * NK + k, gy)
            send(sr.at[it], rr.at[it, z], it, 2, other * NK + k, gy)
        bytes_of(r2.at[it, pl.ds(0, NZ - 1)], rcv.at[it, 1])
        bytes_of(rr.at[it, pl.ds(0, NZ - 1)], rcv.at[it, 2])
        slope = jnp.zeros((2, 8, 128), jnp.float32)
        for n in range(NZ):
            slope = slope + (r2[it, n, 0] - r2[it, n, 1] * (1.0 / (G * n_img + 1)))
        before_q = jnp.zeros((2, 8, 128), jnp.float32)
        norm = before_q
        for n in range(NZ):
            p, q, y0, y1 = (r2[it, n, m] for m in range(4))
            base = (32.0 * n) * slope + before_q
            ud[n, 0], ud[n, 1] = base, slope
            norm = norm + base * (32.0 * base + 1056.0 * slope + 2.0 * y0) + slope * (11440.0 * slope + 2.0 * y1)
            before_q = before_q + q
            slope = slope - p
        row = jnp.sum(norm[0] + norm[1], 0, keepdims=True)
        for n in range(NZ):
            row = row + rr[it, n]
        sa[it] = row
        for n, (dy, dc, dx) in enumerate(NEAR):
            send(sa.at[it], ra.at[it, n], it, 3, z * NK + member(dy, dc), (gy + dx) % NX)
        base, slope = ud[z, 0], ud[z, 1]
        for n in range(NK):
            s3[it, n, 0] = base + (4.0 * n) * slope + ef[n, 0]
            s3[it, n, 1] = slope + ef[n, 1]
        if it < ITERS - 1:
            half = k % 2
            toward = jnp.where(half == 0, below, above)
            for dy, dc in [*PLANE, (0, 0)]:
                other = member(dy, dc)
                send(s3.at[it, other, :, half], r3h.at[k], it, 5, z * NK + other, toward)
        for dy, dc in PLANE:
            other = member(dy, dc)
            send(s3.at[it, other], r3.at[it, k], it, 4, z * NK + other, gy)
        r3[it, k] = s3[it, k]
        bytes_of(r3.at[it, pl.ds(0, NK - 1)], rcv.at[it, 4])
        if it < ITERS - 1:
            bytes_of(r3h, rcv.at[it, 5])
        bytes_of(ra.at[it], rcv.at[it, 3])
        total = sa[it]
        for n in range(len(NEAR)):
            total = total + ra[it, n]
        mean = jnp.maximum(jnp.sum(total, 1, keepdims=True), 0.0) * (1.0 / cells)
        scale = step_length / jnp.sqrt(mean + 1e-06)

        def gathered(n):
            return jnp.concatenate(
                [jnp.concatenate([r3[it, 2 * x, n], r3[it, 2 * x + 1, n]], 0)[None] for x in range(4)], 0
            )

        begin, slope = gathered(0), gathered(1)
        if it == ITERS - 1:
            for i in range(1, G + 1):
                u = begin + float(i) * slope
                if i > 1:
                    u = u + vbuf[i - 2, :, pl.ds(0, 4)]
                out[i - 1] = state[i, :, pl.ds(0, 4)] - scale * u
        else:
            side = [
                jnp.concatenate(
                    [jnp.where(low[0], r3h[2 * x, n][None], r3h[2 * x + 1, n][None])[None] for x in range(4)], 0
                )
                for n in range(2)
            ]
            begin = jnp.concatenate([begin, side[0]], 1)
            slope = jnp.concatenate([slope, side[1]], 1)
            ones = jnp.ones((4, 4, 8, 128), jnp.float32)
            step = scale * jnp.concatenate([ones, inside], 1)
            last = jnp.where(img == n_img - 1, jnp.float32(0.0), jnp.float32(1.0))
            for i in range(G + 2):
                u = begin + float(i) * slope
                if i > 1:
                    u = u + vbuf[i - 2]
                if i == G + 1:
                    u = u * last
                state[i] = state[i] - step * u

    for copy in halo:
        copy.wait_send()
    for it in range(ITERS):
        bytes_of(s1.at[it, pl.ds(0, NK - 1)], snd.at[it, 0])
        bytes_of(r2.at[it, pl.ds(0, NZ - 1)], snd.at[it, 1])
        bytes_of(rr.at[it, pl.ds(0, NZ - 1)], snd.at[it, 2])
        bytes_of(ra.at[it], snd.at[it, 3])
        bytes_of(s3.at[it, pl.ds(0, NK - 1)], snd.at[it, 4])
        if it < ITERS - 1:
            bytes_of(r3h, snd.at[it, 5])


def per_device(path, start_image, end_image, labels, mob_table):
    f32 = jnp.float32
    hbm = pl.BlockSpec(memory_space=pl.ANY)
    vmem = [
        ((G + 2, 4, 4, 8, 128), f32), ((4, 4, 8, 128), jnp.int32), ((2, 4, 4, 8, 128), f32),
        ((G + 2, 4, 8, 128), f32), ((G + 2, 4, 8, 128), f32), ((2, 4, 8, 128), jnp.int32),
        ((G + 2, 4, 5, 8, 128), f32), ((G, 4, 5, 8, 128), f32), ((4, 5, 8, 128), f32),
        ((ITERS, NK, 4, 2, 8, 128), f32), ((ITERS, NK, 4, 2, 8, 128), f32), ((NK, 2, 2, 8, 128), f32),
        ((ITERS, 4, 2, 8, 128), f32), ((ITERS, NZ, 4, 2, 8, 128), f32),
        ((ITERS, 1, 128), f32), ((ITERS, NZ, 1, 128), f32), ((NZ, 2, 2, 8, 128), f32),
        ((ITERS, NK, 2, 2, 8, 128), f32), ((ITERS, NK, 2, 2, 8, 128), f32), ((NK, 2, 8, 128), f32),
        ((ITERS, 1, 128), f32), ((ITERS, len(NEAR), 1, 128), f32),
    ]
    result = pl.pallas_call(
        kernel,
        out_shape=jax.ShapeDtypeStruct((G, 4, 4, 8, 128), f32),
        in_specs=[hbm] * 4 + [pl.BlockSpec(memory_space=pltpu.SMEM)],
        out_specs=pl.BlockSpec(memory_space=pltpu.VMEM),
        scratch_shapes=[pltpu.VMEM(*a) for a in vmem]
        + [
            pltpu.SemaphoreType.DMA((4,)),
            pltpu.SemaphoreType.DMA((10,)),
            pltpu.SemaphoreType.DMA((10,)),
            pltpu.SemaphoreType.DMA((ITERS, 6)),
            pltpu.SemaphoreType.DMA((ITERS, 6)),
        ],
        compiler_params=pltpu.CompilerParams(
            collective_id=0, has_side_effects=True, vmem_limit_bytes=32 * 2**20
        ),
        name="descent",
    )(
        path.reshape(G, 4, 4, 8, 128),
        start_image.reshape(4, 4, 8, 128),
        end_image.reshape(4, 4, 8, 128),
        labels.reshape(4, 4, 8, 128),
        mob_table,
    )
    return result.reshape(path.shape)


def solution(mesh):
    field = P(None, "gy", None)
    return jax.shard_map(
        per_device,
        mesh=mesh,
        in_specs=(P("img", None, "gy", None), field, field, field, P()),
        out_specs=P("img", None, "gy", None),
        check_vma=False,
    )
```

time: 222 us -> 58.8 us (0.26)
  blocking collectives: 132 us -> 0 us
  Pallas kernels: 0 us -> 53.7 us
  starting transfers between devices: 42 us -> 0 us
  waiting for transfers between devices: 23 us -> 0 us
  other arithmetic: 14.5 us -> 0 us
    psum x8 -> x0, blocking collectives: 73.4 us -> none  [by_axis(): return functools.reduce(lax.psum, axes, shard)]
    all_to_all x3 -> x0, blocking collectives: 58.9 us -> none  [the longest x2 35.3 us: per_device(): back = lax.all_to_all(solved, IMG, split_axis=0, concat_axis=1, tiled=True)]
    pallas_call x0 -> x1, Pallas kernels: none -> 53.7 us  [per_device(): pl.pallas_call(kernel, out_shape=jax.ShapeDtypeStruct((G, 4, 4, 8, 128),...]
    ppermute x10 -> x0, starting transfers between devices: 28.4 us -> none  [the longest x4 14.3 us: shifted(): return lax.ppermute(block, axis, route)]
    all_to_all x1 -> x0, starting transfers between devices: 13.6 us -> none  [per_device(): columns = lax.all_to_all(flat, IMG, split_axis=1, concat_axis=0, tiled=True)]
    all_to_all x1 -> x0, waiting for transfers between devices: 13.2 us -> none  [per_device(): columns = lax.all_to_all(flat, IMG, split_axis=1, concat_axis=0, tiled=True)]
    ppermute x10 -> x0, waiting for transfers between devices: 9.86 us -> none  [the longest x4 6.59 us: shifted(): return lax.ppermute(block, axis, route)]
    mul x8 -> x0, other arithmetic: 4.87 us -> none  [the longest x2 3.69 us: per_device(): time_step * time_step * (index * coeff[None] - index * before_g + before_q)]
  transfers between devices with their start and end apart: 11 -> 0, of which waited for: 6 -> 0; matrix products, arithmetic and copies ran while one was open for 2% -> 0% of each run, Pallas kernels for 0% -> 0%
where the time goes in v1:
time: 58.8 us; the launch traced here: 58.5 us
  Pallas kernels  53.7 us (91%)
  local copies, waits for them, and re-layouts  4.83 us (8%)
    pallas_call x1, Pallas kernels, per_device(): pl.pallas_call(kernel, out_shape=jax.ShapeDtypeStruct((G, 4, 4, 8, 128),...  53.7 us
    unnamed x11, local copies, waits for them, and re-layouts  4.83 us

profile of v1, /device:TPU:1, one launch (start us, length us, event | category | flops | bytes accessed | tf_op | source)
XLA Modules:
  0.0 58.5 jit_solution(7073218898096518519)
XLA Ops:
  0.0 0.0 copy-start.4
  0.0 0.7 %copy-done.4 = f32[4]{0:T(128)S(1)} copy-done((f32[4]{0:T(128)S(1)}, f32[4]{0:T(128)}, u32[]{:S(2)}) %copy-start.4) | copy-done | bytes 40
  0.7 0.0 copy-start
  0.7 0.9 %copy-done = f32[4,4,32,128]{3,2,1,0:T(8,128)S(1)} copy-done((f32[4,4,32,128]{3,2,1,0:T(8,128)S(1)}, f32[4,4,32,128]{3,2,1,0:T(8,128)}, u32[]{:S(2)}) %copy-start) | copy-done | bytes 262168
  1.6 0.0 copy-start.1
  1.6 0.8 %copy-done.1 = f32[4,32,128]{2,1,0:T(8,128)S(1)} copy-done((f32[4,32,128]{2,1,0:T(8,128)S(1)}, f32[4,32,128]{2,1,0:T(8,128)}, u32[]{:S(2)}) %copy-start.1) | copy-done | bytes 65560
  2.4 0.0 copy-start.2
  2.4 0.8 %copy-done.2 = f32[4,32,128]{2,1,0:T(8,128)S(1)} copy-done((f32[4,32,128]{2,1,0:T(8,128)S(1)}, f32[4,32,128]{2,1,0:T(8,128)}, u32[]{:S(2)}) %copy-start.2) | copy-done | bytes 65560
  3.3 0.0 copy-start.3
  3.3 0.8 %copy-done.3 = s32[4,32,128]{2,1,0:T(8,128)S(1)} copy-done((s32[4,32,128]{2,1,0:T(8,128)S(1)}, s32[4,32,128]{2,1,0:T(8,128)}, u32[]{:S(2)}) %copy-start.3) | copy-done | bytes 65560
  4.1 53.7 %descent.1 = f32[4,4,4,8,128]{4,3,2,1,0:T(8,128)S(1)} custom-call(f32[4,4,4,8,128]{4,3,2,1,0:T(8,128)S(1)} %bitcast.6, f32[4,4,8,128]{3,2,1,0:T(8,128)S(1)} %bitcast.7, f32[4,4,8,128]{3,2,1,0:T(8,128)S(1)} %bitcast.8, s32[4,4,8,128]{3,2,1,0:T(8,128)S(1)} %bitcast.9, f32[4]{0:T(128)S(1)} %copy-done.4), custom_call_target="tpu_custom_call" | custom-call | tf_op jit(solution)/shard_map/descent/pallas_call | solution.py:303
  57.8 0.7 %copy.7 = f32[4,4,32,128]{3,2,1,0:T(8,128)} copy(f32[4,4,32,128]{3,2,1,0:T(8,128)S(1)} %bitcast.5) | data formatting | bytes 524288
Async XLA Ops:
  0.0 0.7 %copy-start.4 = (f32[4]{0:T(128)S(1)}, f32[4]{0:T(128)}, u32[]{:S(2)}) copy-start(f32[4]{0:T(128)} %table.1) | copy-start | bytes 52
  0.7 0.9 %copy-start = (f32[4,4,32,128]{3,2,1,0:T(8,128)S(1)}, f32[4,4,32,128]{3,2,1,0:T(8,128)}, u32[]{:S(2)}) copy-start(f32[4,4,32,128]{3,2,1,0:T(8,128)} %param.5) | copy-start | bytes 786436
  1.6 0.8 %copy-start.1 = (f32[4,32,128]{2,1,0:T(8,128)S(1)}, f32[4,32,128]{2,1,0:T(8,128)}, u32[]{:S(2)}) copy-start(f32[4,32,128]{2,1,0:T(8,128)} %param.6) | copy-start | bytes 196612
  2.4 0.8 %copy-start.2 = (f32[4,32,128]{2,1,0:T(8,128)S(1)}, f32[4,32,128]{2,1,0:T(8,128)}, u32[]{:S(2)}) copy-start(f32[4,32,128]{2,1,0:T(8,128)} %param.7) | copy-start | bytes 196612
  3.3 0.8 %copy-start.3 = (s32[4,32,128]{2,1,0:T(8,128)S(1)}, s32[4,32,128]{2,1,0:T(8,128)}, u32[]{:S(2)}) copy-start(s32[4,32,128]{2,1,0:T(8,128)} %param.8) | copy-start | bytes 196612

commit v2 on v1

v2 whole, which is shorter than its diff:
```python
import jax
import jax.numpy as jnp
from jax import lax
from jax.experimental import pallas as pl
from jax.experimental.pallas import tpu as pltpu
from jax.sharding import PartitionSpec as P

ITERS = 2
NZ, NK, NX = 8, 8, 4
G = 4
stiffness = 0.25
step_length = 0.05
MESH = pl.DeviceIdType.MESH


def ring(n, d):
    return min(d % n, -d % n)


PLANE = sorted(
    [(dy, dc) for dy in range(4) for dc in range(2) if dy or dc], key=lambda o: (-ring(4, o[0]), -o[1])
)
ZS = sorted(range(1, NZ), key=lambda d: -ring(NZ, d))
NEAR = sorted(
    [(dy, dc, dx) for dy in range(4) for dc in range(2) for dx in range(NX) if dy or dc or dx],
    key=lambda o: (-ring(4, o[0]) - ring(4, o[2]), -o[1]),
)


def six(v, sub):
    total = jnp.concatenate([v[1:], v[:1]], 0) + jnp.concatenate([v[-1:], v[:-1]], 0)
    total = total + pltpu.roll(v, 1, 3) + pltpu.roll(v, 127, 3)
    up = pltpu.roll(v, 7, 2)
    total = total + jnp.where(sub == 7, jnp.concatenate([up[:, 1:], up[:, :1]], 1), up)
    down = pltpu.roll(v, 1, 2)
    return total + jnp.where(sub == 0, jnp.concatenate([down[:, -1:], down[:, :-1]], 1), down)


def kernel(
    path, start, end, labels, levels, out,
    own, lab, edge, nxt, prv, labx, state, ubuf, mobb, made,
    s1, r1, ef, s2, r2, sr, rr, ud, s3, r3, r3h, sa, ra,
    table, loc, init_s, init_r, snd, rcv,
):
    img, gy = lax.axis_index("img"), lax.axis_index("gy")
    z, k = img // NK, img % NK
    y, c = k // 2, k % 2
    n_img = NZ * NK
    right, left = (img + 1) % n_img, (img + n_img - 1) % n_img
    above, below = (gy + 1) % NX, (gy + NX - 1) % NX

    def member(dy, dc):
        return ((y + dy) % 4) * 2 + (c + dc) % 2

    local = [
        pltpu.make_async_copy(path, own.at[pl.ds(0, G)], loc.at[0]),
        pltpu.make_async_copy(start, own.at[G], loc.at[1]),
        pltpu.make_async_copy(end, own.at[G + 1], loc.at[2]),
        pltpu.make_async_copy(labels, lab, loc.at[3]),
        pltpu.make_async_copy(levels, table, loc.at[4]),
    ]
    for copy in local:
        copy.start()

    barrier = pltpu.get_barrier_semaphore()

    def greet(i, x):
        pl.semaphore_signal(barrier, inc=1, device_id=(i, x), device_id_type=MESH)

    for d in ZS:
        greet(((z + d) % NZ) * NK + k, gy)
    for dy, dc, dx in NEAR:
        greet(z * NK + member(dy, dc), (gy + dx) % NX)

    @pl.when(k == 0)
    def _():
        for x in (gy, above, below):
            greet(left, x)

    @pl.when(k == NK - 1)
    def _():
        for x in (gy, above, below):
            greet(right, x)

    at_end = jnp.where((k == 0) | (k == NK - 1), 3, 0)
    for copy in local:
        copy.wait()
    pl.semaphore_wait(barrier, len(ZS) + len(NEAR) + at_end)

    to_right = jnp.where(img == n_img - 1, G, G - 1)
    to_left = jnp.where(img == 0, G + 1, 0)
    moves = [
        (own.at[to_right], edge.at[0], right, gy),
        (own.at[to_left], edge.at[1], left, gy),
        (own.at[to_right, :, 3], prv.at[0], right, above),
        (own.at[to_right, :, 0], nxt.at[0], right, below),
        (own.at[to_left, :, 3], prv.at[G + 1], left, above),
        (own.at[to_left, :, 0], nxt.at[G + 1], left, below),
        (lab.at[:, 3], labx.at[0], img, above),
        (lab.at[:, 0], labx.at[1], img, below),
        (own.at[pl.ds(0, G), :, 3], prv.at[pl.ds(1, G)], img, above),
        (own.at[pl.ds(0, G), :, 0], nxt.at[pl.ds(1, G)], img, below),
    ]
    halo = [
        pltpu.make_async_remote_copy(a, b, init_s.at[n], init_r.at[n], device_id=(i, x), device_id_type=MESH)
        for n, (a, b, i, x) in enumerate(moves)
    ]
    for copy in halo:
        copy.start()

    shape = (4, 5, 8, 128)
    sub = lax.broadcasted_iota(jnp.int32, shape, 2)
    low = lax.broadcasted_iota(jnp.int32, (4, 1, 8, 128), 2) < 4
    has_next = jnp.where(gy < NX - 1, jnp.float32(1.0), jnp.float32(0.0))
    has_prev = jnp.where(gy > 0, jnp.float32(1.0), jnp.float32(0.0))
    inside = jnp.where(low, has_next, has_prev)

    def arrived(names):
        for n in names:
            halo[n].wait_recv()

    def fill(i):
        centre = edge[0] if i == 0 else edge[1] if i == G + 1 else own[i - 1]
        side = jnp.where(low, nxt[i][:, None], prv[i][:, None]) * inside
        state[i] = jnp.concatenate([centre, side], 1)

    def send(src, dst, it, n, i, x):
        copy = pltpu.make_async_remote_copy(
            src, dst, snd.at[it, n], rcv.at[it, n], device_id=(i, x), device_id_type=MESH
        )
        copy.start()

    def bytes_of(ref, sem):
        pltpu.make_async_copy(ref, ref, sem).wait()

    def force(i):
        p = state[i]
        return mobb[...] * (stiffness * six(p, sub) - p * (0.5 + p * p))

    def residual(i, f):
        return (state[i + 1] - state[i]) * 2.0 - f

    def quarter(i, before, r):
        p = state[i]
        m = mobb[...] * r
        return 0.5 * (before - r) + ((0.125 + 0.75 * p * p) * m - 0.0625 * six(m, sub))

    cells = n_img * G * 4 * 32 * NX * 128
    zero = jnp.zeros((2, 8, 128), jnp.float32)
    for it in range(ITERS):
        if it == 0:
            arrived((6, 7))
            every = jnp.concatenate([lab[...], jnp.where(low, labx[1][:, None], labx[0][:, None])], 1)
            mob = jnp.zeros(shape, jnp.float32)
            for level in range(4):
                mob = jnp.where(every == level, table[level], mob)
            mobb[...] = jnp.concatenate([mob[:, :4], mob[:, 4:] * inside], 1)
            arrived((8, 9))
            for i in range(1, G + 1):
                fill(i)
        ra1 = residual(1, force(1))
        ra2 = residual(2, force(2))
        ra3 = residual(3, force(3))
        h2 = quarter(2, ra1, ra2)
        h3 = quarter(3, ra2, ra3)
        f4 = force(4)
        if it == 0:
            made[0], made[1], made[2], made[3], made[4] = ra1, ra3, h2, h3, f4
            arrived((1, 4, 5))
            fill(G + 1)
            arrived((0, 2, 3))
            fill(0)
            ra1, ra3, h2, h3, f4 = (made[n] for n in range(5))
        h4 = quarter(4, ra3, residual(4, f4))
        h1 = quarter(1, residual(0, force(0)), ra1)
        for n, v in enumerate((h1 + h2 + h3 + h4, h1 + 2.0 * h2 + 3.0 * h3 + 4.0 * h4)):
            for share in range(NK):
                t = (share % 2) * 2
                s1[it, share, n] = v[share // 2, t : t + 2]
        for dy, dc in PLANE:
            other = member(dy, dc)
            send(s1.at[it, other, pl.ds(0, 2)], r1.at[it, k, pl.ds(0, 2)], it, 0, z * NK + other, gy)
        v2 = -h1
        v3 = 2.0 * v2 - h2
        v4 = 2.0 * v3 - v2 - h3
        for n, v in enumerate((v2 + v3 + v4, 2.0 * v2 + 3.0 * v3 + 4.0 * v4)):
            for share in range(NK):
                t = (share % 2) * 2
                s1[it, share, 2 + n] = v[share // 2, t : t + 2]
        for dy, dc in PLANE:
            other = member(dy, dc)
            send(s1.at[it, other, pl.ds(2, 2)], r1.at[it, k, pl.ds(2, 2)], it, 1, z * NK + other, gy)
        r1[it, k] = s1[it, k]
        ubuf[2], ubuf[3], ubuf[4] = v2, v3, v4
        ubuf[5] = 2.0 * v4 - v3 - h4
        squares = (v2 * v2 + v3 * v3 + v4 * v4)[:, :4]
        squares = jnp.sum(jnp.sum(squares, 0), 0)

        bytes_of(r1.at[it, pl.ds(0, NK - 1), pl.ds(0, 2)], rcv.at[it, 0])
        sum_p, sum_q = zero, zero
        for n in range(NK):
            p, q = r1[it, n, 0], r1[it, n, 1]
            ef[n, 0], ef[n, 1] = sum_q - (4.0 * n) * sum_p, -sum_p
            sum_q = sum_q + (4.0 * n) * p + q
            sum_p = sum_p + p
        first = (z * (G * NK)).astype(jnp.float32)
        for n, v in enumerate((sum_p, sum_q + first * sum_p)):
            s2[it, n] = v
            r2[it, z, n] = v
        for d in ZS:
            other = (z + d) % NZ
            send(s2.at[it, pl.ds(0, 2)], r2.at[it, z, pl.ds(0, 2)], it, 2, other * NK + k, gy)

        bytes_of(r1.at[it, pl.ds(0, NK - 1), pl.ds(2, 2)], rcv.at[it, 1])
        y0, y1, y2 = zero, zero, zero
        for n in range(NK):
            e, f, w0, w1 = ef[n, 0], ef[n, 1], r1[it, n, 2], r1[it, n, 3]
            y0 = y0 + 4.0 * e + 10.0 * f + w0
            y1 = y1 + (16.0 * n + 10.0) * e + (40.0 * n + 30.0) * f + (4.0 * n) * w0 + w1
            y2 = y2 + e * (4.0 * e + 20.0 * f + 2.0 * w0) + f * (30.0 * f + 2.0 * w1)
        for n, v in enumerate((y0, y1)):
            s2[it, 2 + n] = v
            r2[it, z, 2 + n] = v
        row = jnp.sum(y2[0] + y2[1] + squares, 0, keepdims=True)
        sr[it] = row
        rr[it, z] = row
        for d in ZS:
            other = (z + d) % NZ
            send(s2.at[it, pl.ds(2, 2)], r2.at[it, z, pl.ds(2, 2)], it, 3, other * NK + k, gy)
            send(sr.at[it], rr.at[it, z], it, 4, other * NK + k, gy)

        bytes_of(r2.at[it, pl.ds(0, NZ - 1), pl.ds(0, 2)], rcv.at[it, 2])
        slope = zero
        for n in range(NZ):
            slope = slope + (r2[it, n, 0] - r2[it, n, 1] * (1.0 / (G * n_img + 1)))
        sum_q = zero
        for n in range(NZ):
            ud[n, 0], ud[n, 1] = (32.0 * n) * slope + sum_q, slope
            sum_q = sum_q + r2[it, n, 1]
            slope = slope - r2[it, n, 0]
        base, slope = ud[z, 0], ud[z, 1]
        for n in range(NK):
            s3[it, n, 0] = base + (4.0 * n) * slope + ef[n, 0]
            s3[it, n, 1] = slope + ef[n, 1]
        if it < ITERS - 1:
            half = k % 2
            toward = jnp.where(half == 0, below, above)
            for dy, dc in [*PLANE, (0, 0)]:
                other = member(dy, dc)
                send(s3.at[it, other, :, half], r3h.at[k], it, 7, z * NK + other, toward)
        for dy, dc in PLANE:
            other = member(dy, dc)
            send(s3.at[it, other], r3.at[it, k], it, 6, z * NK + other, gy)
        r3[it, k] = s3[it, k]

        bytes_of(r2.at[it, pl.ds(0, NZ - 1), pl.ds(2, 2)], rcv.at[it, 3])
        norm = zero
        for n in range(NZ):
            base, slope = ud[n, 0], ud[n, 1]
            norm = norm + base * (32.0 * base + 1056.0 * slope + 2.0 * r2[it, n, 2])
            norm = norm + slope * (11440.0 * slope + 2.0 * r2[it, n, 3])
        row = jnp.sum(norm[0] + norm[1], 0, keepdims=True)
        bytes_of(rr.at[it, pl.ds(0, NZ - 1)], rcv.at[it, 4])
        for n in range(NZ):
            row = row + rr[it, n]
        sa[it] = row
        for n, (dy, dc, dx) in enumerate(NEAR):
            send(sa.at[it], ra.at[it, n], it, 5, z * NK + member(dy, dc), (gy + dx) % NX)

        bytes_of(r3.at[it, pl.ds(0, NK - 1)], rcv.at[it, 6])

        def gathered(n):
            return jnp.concatenate(
                [jnp.concatenate([r3[it, 2 * x, n], r3[it, 2 * x + 1, n]], 0)[None] for x in range(4)], 0
            )

        begin, slope = gathered(0), gathered(1)
        if it == ITERS - 1:
            for i in range(1, G + 1):
                u = begin + float(i) * slope
                if i > 1:
                    u = u + ubuf[i, :, pl.ds(0, 4)]
                ubuf[i, :, pl.ds(0, 4)] = u
        else:
            bytes_of(r3h, rcv.at[it, 7])
            side = [
                jnp.concatenate(
                    [jnp.where(low[0], r3h[2 * x, n][None], r3h[2 * x + 1, n][None])[None] for x in range(4)], 0
                )
                * inside
                for n in range(2)
            ]
            begin = jnp.concatenate([begin, side[0]], 1)
            slope = jnp.concatenate([slope, side[1]], 1)
            last = jnp.where(img == n_img - 1, jnp.float32(0.0), jnp.float32(1.0))
            for i in range(G + 2):
                u = begin + float(i) * slope
                if i > 1:
                    v = ubuf[i]
                    u = u + jnp.concatenate([v[:, :4], v[:, 4:] * inside], 1)
                if i == G + 1:
                    u = u * last
                ubuf[i] = u

        bytes_of(ra.at[it], rcv.at[it, 5])
        total = sa[it]
        for n in range(len(NEAR)):
            total = total + ra[it, n]
        mean = jnp.maximum(jnp.sum(total, 1, keepdims=True), 0.0) * (1.0 / cells)
        scale = step_length / jnp.sqrt(mean + 1e-06)
        if it == ITERS - 1:
            for i in range(1, G + 1):
                out[i - 1] = state[i, :, pl.ds(0, 4)] - scale * ubuf[i, :, pl.ds(0, 4)]
        else:
            for i in range(G + 2):
                state[i] = state[i] - scale * ubuf[i]

    for copy in halo:
        copy.wait_send()
    for it in range(ITERS):
        bytes_of(s1.at[it, pl.ds(0, NK - 1), pl.ds(0, 2)], snd.at[it, 0])
        bytes_of(s1.at[it, pl.ds(0, NK - 1), pl.ds(2, 2)], snd.at[it, 1])
        bytes_of(r2.at[it, pl.ds(0, NZ - 1), pl.ds(0, 2)], snd.at[it, 2])
        bytes_of(r2.at[it, pl.ds(0, NZ - 1), pl.ds(2, 2)], snd.at[it, 3])
        bytes_of(rr.at[it, pl.ds(0, NZ - 1)], snd.at[it, 4])
        bytes_of(ra.at[it], snd.at[it, 5])
        bytes_of(s3.at[it, pl.ds(0, NK - 1)], snd.at[it, 6])
        if it < ITERS - 1:
            bytes_of(r3h, snd.at[it, 7])


def per_device(path, start_image, end_image, labels, mob_table):
    f32 = jnp.float32
    hbm = pl.BlockSpec(memory_space=pltpu.HBM)
    vmem = [
        ((G + 2, 4, 4, 8, 128), f32), ((4, 4, 8, 128), jnp.int32), ((2, 4, 4, 8, 128), f32),
        ((G + 2, 4, 8, 128), f32), ((G + 2, 4, 8, 128), f32), ((2, 4, 8, 128), jnp.int32),
        ((G + 2, 4, 5, 8, 128), f32), ((G + 2, 4, 5, 8, 128), f32), ((4, 5, 8, 128), f32),
        ((5, 4, 5, 8, 128), f32),
        ((ITERS, NK, 4, 2, 8, 128), f32), ((ITERS, NK, 4, 2, 8, 128), f32), ((NK, 2, 2, 8, 128), f32),
        ((ITERS, 4, 2, 8, 128), f32), ((ITERS, NZ, 4, 2, 8, 128), f32),
        ((ITERS, 1, 128), f32), ((ITERS, NZ, 1, 128), f32), ((NZ, 2, 2, 8, 128), f32),
        ((ITERS, NK, 2, 2, 8, 128), f32), ((ITERS, NK, 2, 2, 8, 128), f32), ((NK, 2, 8, 128), f32),
        ((ITERS, 1, 128), f32), ((ITERS, len(NEAR), 1, 128), f32),
    ]
    result = pl.pallas_call(
        kernel,
        out_shape=jax.ShapeDtypeStruct((G, 4, 4, 8, 128), f32),
        in_specs=[hbm] * 5,
        out_specs=pl.BlockSpec(memory_space=pltpu.VMEM),
        scratch_shapes=[pltpu.VMEM(*a) for a in vmem]
        + [
            pltpu.SMEM((4,), f32),
            pltpu.SemaphoreType.DMA((5,)),
            pltpu.SemaphoreType.DMA((10,)),
            pltpu.SemaphoreType.DMA((10,)),
            pltpu.SemaphoreType.DMA((ITERS, 8)),
            pltpu.SemaphoreType.DMA((ITERS, 8)),
        ],
        compiler_params=pltpu.CompilerParams(
            collective_id=0, has_side_effects=True, vmem_limit_bytes=32 * 2**20
        ),
        name="descent",
    )(
        *(
            pltpu.with_memory_space_constraint(v, pltpu.HBM)
            for v in (
                path.reshape(G, 4, 4, 8, 128),
                start_image.reshape(4, 4, 8, 128),
                end_image.reshape(4, 4, 8, 128),
                labels.reshape(4, 4, 8, 128),
                mob_table,
            )
        )
    )
    return result.reshape(path.shape)


def solution(mesh):
    field = P(None, "gy", None)
    return jax.shard_map(
        per_device,
        mesh=mesh,
        in_specs=(P("img", None, "gy", None), field, field, field, P()),
        out_specs=P("img", None, "gy", None),
        check_vma=False,
    )
```

time: 58.8 us -> 51.7 us (0.88)
  local copies, waits for them, and re-layouts: 4.83 us -> 0.71 us
  Pallas kernels: 53.7 us -> 50.9 us
    unnamed x11 -> x1, local copies, waits for them, and re-layouts: 4.83 us -> 0.71 us
    pallas_call x1, Pallas kernels: 53.7 us -> 50.9 us  [per_device(): pl.pallas_call(kernel, out_shape=jax.ShapeDtypeStruct((G, 4, 4, 8, 128),...]
where the time goes in v2:
time: 51.7 us; the launch traced here: 51.6 us
  Pallas kernels  50.9 us (98%)
  local copies, waits for them, and re-layouts  0.71 us (1%)
    pallas_call x1, Pallas kernels, per_device(): pl.pallas_call(kernel, out_shape=jax.ShapeDtypeStruct((G, 4, 4, 8, 128),...  50.9 us

profile of v2, /device:TPU:1, one launch (start us, length us, event | category | flops | bytes accessed | tf_op | source)
XLA Modules:
  0.0 51.6 jit_solution(12283192508395140955)
XLA Ops:
  0.0 50.9 %descent.1 = f32[4,4,4,8,128]{4,3,2,1,0:T(8,128)S(1)} custom-call(f32[4,4,4,8,128]{4,3,2,1,0:T(8,128)} %bitcast.6, f32[4,4,8,128]{3,2,1,0:T(8,128)} %bitcast.7, f32[4,4,8,128]{3,2,1,0:T(8,128)} %bitcast.8, s32[4,4,8,128]{3,2,1,0:T(8,128)} %bitcast.9, f32[4]{0:T(128)} %levels.1), custom_call_target="tpu_custom_call" | custom-call | tf_op jit(solution)/shard_map/descent/pallas_call | solution.py:346
  50.9 0.7 %copy.7 = f32[4,4,32,128]{3,2,1,0:T(8,128)} copy(f32[4,4,32,128]{3,2,1,0:T(8,128)S(1)} %bitcast.5) | data formatting | bytes 524288

commit v3 on v2

v3 whole, which is shorter than its diff:
```python
import jax
import jax.numpy as jnp
from jax import lax
from jax.experimental import pallas as pl
from jax.experimental.pallas import tpu as pltpu
from jax.sharding import PartitionSpec as P

ITERS = 2
NZ, NK, NX = 4, 16, 4
G = 4
SPAN = G * NK
stiffness = 0.25
step_length = 0.05
MESH = pl.DeviceIdType.MESH


def ring(n, d):
    return min(d % n, -d % n)


MEMBERS = [(dz, dy, dc) for dz in range(2) for dy in range(4) for dc in range(2)]
PLANE = sorted([m for m in MEMBERS if any(m)], key=lambda o: (-o[0] - ring(4, o[1]), -o[2]))
ZS = sorted(range(1, NZ), key=lambda d: -ring(NZ, d))
NEAR = sorted(
    [(*m, dx) for m in MEMBERS for dx in range(NX) if any(m) or dx],
    key=lambda o: (-o[0] - ring(4, o[1]) - ring(4, o[3]), -o[2]),
)


def six(ref, i, x, sub):
    v = ref[i, x]
    total = ref[i, (x + 1) % 4] + ref[i, (x + 3) % 4]
    total = total + pltpu.roll(v, 1, 2) + pltpu.roll(v, 127, 2)
    up = pltpu.roll(v, 7, 1)
    total = total + jnp.where(sub == 7, jnp.concatenate([up[1:], up[:1]], 0), up)
    down = pltpu.roll(v, 1, 1)
    return v, total + jnp.where(sub == 0, jnp.concatenate([down[-1:], down[:-1]], 0), down)


def kernel(
    path, start, end, labels, levels, out,
    own, lab, edge, nxt, prv, labx, state, ubuf, mobb, res, mres,
    s1, r1, ef, s2, r2, ud, s3, r3, r3h, sa, ra,
    table, loc, init_s, init_r, snd, rcv, relay,
):
    img, gy = lax.axis_index("img"), lax.axis_index("gy")
    z, k = img // NK, img % NK
    pair, y, c = k // 8, (k // 2) % 4, k % 2
    n_img = NZ * NK
    right, left = (img + 1) % n_img, (img + n_img - 1) % n_img
    above, below = (gy + 1) % NX, (gy + NX - 1) % NX

    def member(dz, dy, dc):
        return ((pair + dz) % 2) * 8 + ((y + dy) % 4) * 2 + (c + dc) % 2

    barrier = pltpu.get_barrier_semaphore()

    def signal(sem, i, x):
        pl.semaphore_signal(sem, inc=1, device_id=(i, x), device_id_type=MESH)

    def along_z(d):
        return ((z + d) % NZ) * NK + k

    for i in (left, right):
        for x in (above, below):
            signal(barrier, i, x)
    for d in (1, NZ - 1):
        signal(barrier, along_z(d), gy)

    @pl.when(k == 0)
    def _():
        signal(barrier, left, gy)

    @pl.when(k == NK - 1)
    def _():
        signal(barrier, right, gy)

    for x in (above, below):
        signal(barrier, img, x)
    for m in PLANE:
        signal(barrier, z * NK + member(*m), gy)

    local = [
        pltpu.make_async_copy(labels, lab, loc.at[0]),
        pltpu.make_async_copy(path, own, loc.at[1]),
        pltpu.make_async_copy(levels, table, loc.at[2]),
    ]
    for copy in local:
        copy.start()
    pl.semaphore_wait(barrier, len(PLANE) + 8 + jnp.where((k == 0) | (k == NK - 1), 1, 0))

    def halo_of(n, src, dst, i, x):
        return pltpu.make_async_remote_copy(
            src, dst, init_s.at[n], init_r.at[n], device_id=(i, x), device_id_type=MESH
        )

    def images(image, slot, i, n):
        return [
            halo_of(n, image, edge.at[min(slot, 1)], i, gy),
            halo_of(n + 1, image.at[:, 3], prv.at[slot], i, above),
            halo_of(n + 2, image.at[:, 0], nxt.at[slot], i, below),
        ]

    def begin_of(copies):
        for copy in copies:
            copy.start()

    halo = [*images(path.at[G - 1], 0, right, 0), *images(path.at[0], G + 1, left, 3)]
    halo += [
        halo_of(6, labels.at[:, 3], labx.at[0], img, above),
        halo_of(7, labels.at[:, 0], labx.at[1], img, below),
        halo_of(8, path.at[:, :, 3], prv.at[pl.ds(1, G)], img, above),
        halo_of(9, path.at[:, :, 0], nxt.at[pl.ds(1, G)], img, below),
    ]
    begin_of(halo[6:])

    @pl.when(img != n_img - 1)
    def _():
        begin_of(halo[:3])

    @pl.when(img == n_img - 1)
    def _():
        begin_of(images(start, 0, right, 0))

    @pl.when(img != 0)
    def _():
        begin_of(halo[3:6])

    @pl.when(img == 0)
    def _():
        begin_of(images(end, G + 1, left, 3))

    for i, x in ((along_z(1), gy), (along_z(NZ - 1), gy), (img, above), (img, below)):
        signal(relay.at[0], i, x)
    for copy in local:
        copy.wait()

    shape = (4, 5, 8, 128)
    sub = lax.broadcasted_iota(jnp.int32, (5, 8, 128), 1)
    low = lax.broadcasted_iota(jnp.int32, (4, 1, 8, 128), 2) < 4
    has_next = jnp.where(gy < NX - 1, jnp.float32(1.0), jnp.float32(0.0))
    has_prev = jnp.where(gy > 0, jnp.float32(1.0), jnp.float32(0.0))
    inside = jnp.where(low, has_next, has_prev)

    def arrived(names):
        for n in names:
            halo[n].wait_recv()

    def fill(i):
        centre = edge[0] if i == 0 else edge[1] if i == G + 1 else own[i - 1]
        side = jnp.where(low, nxt[i][:, None], prv[i][:, None]) * inside
        state[i] = jnp.concatenate([centre, side], 1)

    def send(src, dst, it, n, i, x):
        copy = pltpu.make_async_remote_copy(
            src, dst, snd.at[it, n], rcv.at[it, n], device_id=(i, x), device_id_type=MESH
        )
        copy.start()

    def bytes_of(ref, sem):
        pltpu.make_async_copy(ref, ref, sem).wait()

    def force(i, x):
        p, total = six(state, i, x, sub)
        return p, mobb[x] * (stiffness * total - p * (0.5 + p * p))

    def keep(i, x, p, f):
        r = (state[i + 1, x] - p) * 2.0 - f
        res[i, x] = r
        if i:
            mres[i, x] = mobb[x] * r

    def quarter(i, x):
        p = state[i, x]
        m, total = six(mres, i, x, sub)
        return 0.5 * (res[i - 1, x] - res[i, x]) + ((0.125 + 0.75 * p * p) * m - 0.0625 * total)

    cells = n_img * G * 4 * 32 * NX * 128
    zero = jnp.zeros((8, 128), jnp.float32)
    for it in range(ITERS):
        if it == 0:
            arrived((6, 7))
            every = jnp.concatenate([lab[...], jnp.where(low, labx[1][:, None], labx[0][:, None])], 1)
            mob = jnp.zeros(shape, jnp.float32)
            for level in range(4):
                mob = jnp.where(every == level, table[level], mob)
            mobb[...] = jnp.concatenate([mob[:, :4], mob[:, 4:] * inside], 1)
            arrived((8, 9))
            for i in range(1, G + 1):
                fill(i)
        for i in range(1, G):
            for x in range(4):
                keep(i, x, *force(i, x))
        for x in range(4):
            res[G, x] = force(G, x)[1]
        if it == 0:
            arrived((1, 2, 0))
            fill(0)
        for x in range(4):
            keep(0, x, *force(0, x))
        if it == 0:
            arrived((4, 5, 3))
            fill(G + 1)
            pl.semaphore_wait(relay.at[0], 4)
            for i, x in ((img, above), (img, below)):
                signal(relay.at[1], i, x)
        for x in range(4):
            keep(G, x, state[G, x], res[G, x])
        squares = jnp.zeros((4, 8, 128), jnp.float32)
        for turn in (2, 3, 1, 0):
            x = (k // 4 + turn) % 4
            h1, h2, h3, h4 = (quarter(i, x) for i in range(1, G + 1))
            v2 = -h1
            v3 = 2.0 * v2 - h2
            v4 = 2.0 * v3 - v2 - h3
            sums = (
                h1 + h2 + h3 + h4,
                h1 + 2.0 * h2 + 3.0 * h3 + 4.0 * h4,
                v2 + v3 + v4,
                2.0 * v2 + 3.0 * v3 + 4.0 * v4,
            )
            for n, v in enumerate(sums):
                for t in range(4):
                    s1[it, 4 * x + t, n] = v[t]
            for t in range(4):
                if turn or t:
                    other = 4 * x + (k + t) % 4
                    send(s1.at[it, other, pl.ds(0, 2)], r1.at[it, k, pl.ds(0, 2)], it, 0, z * NK + other, gy)
            ubuf[2, x], ubuf[3, x], ubuf[4, x], ubuf[5, x] = v2, v3, v4, 2.0 * v4 - v3 - h4
            squares = squares + (v2 * v2 + v3 * v3 + v4 * v4)[:4]
        for m in PLANE:
            other = member(*m)
            send(s1.at[it, other, pl.ds(2, 2)], r1.at[it, k, pl.ds(2, 2)], it, 1, z * NK + other, gy)
        r1[it, k] = s1[it, k]
        squares = jnp.sum(squares, 0)

        bytes_of(r1.at[it, pl.ds(0, NK - 1), pl.ds(0, 2)], rcv.at[it, 0])
        sum_p, sum_q = zero, zero
        for n in range(NK):
            p, q = r1[it, n, 0], r1[it, n, 1]
            ef[n, 0], ef[n, 1] = sum_q - (4.0 * n) * sum_p, -sum_p
            sum_q = sum_q + (4.0 * n) * p + q
            sum_p = sum_p + p
        first = (z * SPAN).astype(jnp.float32)
        for n, v in enumerate((sum_p, sum_q + first * sum_p)):
            s2[it, n] = v
            r2[it, z, n] = v
        if it == 0:
            pl.semaphore_wait(relay.at[1], 2)
        for d in ZS:
            other = (z + d) % NZ
            send(s2.at[it, pl.ds(0, 2)], r2.at[it, z, pl.ds(0, 2)], it, 2, other * NK + k, gy)

        bytes_of(r1.at[it, pl.ds(0, NK - 1), pl.ds(2, 2)], rcv.at[it, 1])
        y0, y1, y2 = zero, zero, zero
        for n in range(NK):
            e, f, w0, w1 = ef[n, 0], ef[n, 1], r1[it, n, 2], r1[it, n, 3]
            y0 = y0 + 4.0 * e + 10.0 * f + w0
            y1 = y1 + (16.0 * n + 10.0) * e + (40.0 * n + 30.0) * f + (4.0 * n) * w0 + w1
            y2 = y2 + e * (4.0 * e + 20.0 * f + 2.0 * w0) + f * (30.0 * f + 2.0 * w1)
        for n, v in enumerate((y0, y1, y2 + squares)):
            s2[it, 2 + n] = v
            r2[it, z, 2 + n] = v
        for d in ZS:
            other = (z + d) % NZ
            send(s2.at[it, pl.ds(2, 3)], r2.at[it, z, pl.ds(2, 3)], it, 3, other * NK + k, gy)

        bytes_of(r2.at[it, pl.ds(0, NZ - 1), pl.ds(0, 2)], rcv.at[it, 2])
        slope = zero
        for n in range(NZ):
            slope = slope + (r2[it, n, 0] - r2[it, n, 1] * (1.0 / (G * n_img + 1)))
        sum_q = zero
        for n in range(NZ):
            ud[n, 0], ud[n, 1] = float(SPAN * n) * slope + sum_q, slope
            sum_q = sum_q + r2[it, n, 1]
            slope = slope - r2[it, n, 0]
        base, slope = ud[z, 0], ud[z, 1]
        for n in range(NK):
            s3[it, n, 0] = base + (4.0 * n) * slope + ef[n, 0]
            s3[it, n, 1] = slope + ef[n, 1]
        if it < ITERS - 1:

            @pl.when((k % 4) % 3 == 0)
            def _(it=it):
                low_end = k % 4 == 0
                slot = (k // 4) * 2 + jnp.where(low_end, 0, 1)
                for m in MEMBERS:
                    other = member(*m)
                    send(s3.at[it, other], r3h.at[slot], it, 7, z * NK + other, jnp.where(low_end, below, above))

        for m in PLANE:
            other = member(*m)
            send(s3.at[it, other], r3.at[it, k], it, 6, z * NK + other, gy)
        r3[it, k] = s3[it, k]

        bytes_of(r2.at[it, pl.ds(0, NZ - 1), pl.ds(2, 3)], rcv.at[it, 3])
        norm = zero
        for n in range(NZ):
            base, slope = ud[n, 0], ud[n, 1]
            norm = norm + base * (float(SPAN) * base + float(SPAN * (SPAN + 1)) * slope + 2.0 * r2[it, n, 2])
            norm = norm + slope * (float(SPAN * (SPAN + 1) * (2 * SPAN + 1) // 6) * slope + 2.0 * r2[it, n, 3])
            norm = norm + r2[it, n, 4]
        row = jnp.sum(norm, 0, keepdims=True)
        sa[it] = row
        for n, (*m, dx) in enumerate(NEAR):
            send(sa.at[it], ra.at[it, n], it, 5, z * NK + member(*m), (gy + dx) % NX)

        bytes_of(r3.at[it, pl.ds(0, NK - 1)], rcv.at[it, 6])

        begin, slope = (r3[it, :, n].reshape(4, 4, 8, 128) for n in range(2))
        if it == ITERS - 1:
            for i in range(1, G + 1):
                u = begin + float(i) * slope
                if i > 1:
                    u = u + ubuf[i, :, pl.ds(0, 4)]
                ubuf[i, :, pl.ds(0, 4)] = u
        else:
            bytes_of(r3h, rcv.at[it, 7])
            side = [
                jnp.concatenate(
                    [jnp.where(low[0], r3h[2 * x, n][None], r3h[2 * x + 1, n][None])[None] for x in range(4)], 0
                )
                for n in range(2)
            ]
            begin = jnp.concatenate([begin, side[0]], 1)
            slope = jnp.concatenate([slope, side[1]], 1)
            last = jnp.where(img == n_img - 1, jnp.float32(0.0), jnp.float32(1.0))
            for i in range(G + 2):
                u = begin + float(i) * slope
                if i > 1:
                    u = u + ubuf[i]
                if i == G + 1:
                    u = u * last
                ubuf[i] = u

        bytes_of(ra.at[it], rcv.at[it, 5])
        total = sa[it]
        for n in range(len(NEAR)):
            total = total + ra[it, n]
        mean = jnp.maximum(jnp.sum(total, 1, keepdims=True), 0.0) * (1.0 / cells)
        scale = step_length / jnp.sqrt(mean + 1e-06)
        if it == ITERS - 1:
            for i in range(1, G + 1):
                out[i - 1] = state[i, :, pl.ds(0, 4)] - scale * ubuf[i, :, pl.ds(0, 4)]
        else:
            step = scale * inside
            for i in range(G + 2):
                state[i, :, pl.ds(0, 4)] = state[i, :, pl.ds(0, 4)] - scale * ubuf[i, :, pl.ds(0, 4)]
                state[i, :, pl.ds(4, 1)] = state[i, :, pl.ds(4, 1)] - step * ubuf[i, :, pl.ds(4, 1)]

    for copy in halo:
        copy.wait_send()
    for it in range(ITERS):
        bytes_of(s1.at[it, pl.ds(0, NK - 1), pl.ds(0, 2)], snd.at[it, 0])
        bytes_of(s1.at[it, pl.ds(0, NK - 1), pl.ds(2, 2)], snd.at[it, 1])
        bytes_of(r2.at[it, pl.ds(0, NZ - 1), pl.ds(0, 2)], snd.at[it, 2])
        bytes_of(r2.at[it, pl.ds(0, NZ - 1), pl.ds(2, 3)], snd.at[it, 3])
        bytes_of(ra.at[it], snd.at[it, 5])
        bytes_of(s3.at[it, pl.ds(0, NK - 1)], snd.at[it, 6])
        if it < ITERS - 1:

            @pl.when((k % 4) % 3 == 0)
            def _(it=it):
                bytes_of(s3.at[it], snd.at[it, 7])


def per_device(path, start_image, end_image, labels, mob_table):
    f32 = jnp.float32
    hbm = pl.BlockSpec(memory_space=pltpu.HBM)
    vmem = [
        ((G, 4, 4, 8, 128), f32), ((4, 4, 8, 128), jnp.int32), ((2, 4, 4, 8, 128), f32),
        ((G + 2, 4, 8, 128), f32), ((G + 2, 4, 8, 128), f32), ((2, 4, 8, 128), jnp.int32),
        ((G + 2, 4, 5, 8, 128), f32), ((G + 2, 4, 5, 8, 128), f32), ((4, 5, 8, 128), f32),
        ((G + 1, 4, 5, 8, 128), f32), ((G + 1, 4, 5, 8, 128), f32),
        ((ITERS, NK, 4, 8, 128), f32), ((ITERS, NK, 4, 8, 128), f32), ((NK, 2, 8, 128), f32),
        ((ITERS, 5, 8, 128), f32), ((ITERS, NZ, 5, 8, 128), f32), ((NZ, 2, 8, 128), f32),
        ((ITERS, NK, 2, 8, 128), f32), ((ITERS, NK, 2, 8, 128), f32), ((8, 2, 8, 128), f32),
        ((ITERS, 1, 128), f32), ((ITERS, len(NEAR), 1, 128), f32),
    ]
    result = pl.pallas_call(
        kernel,
        out_shape=jax.ShapeDtypeStruct((G, 4, 4, 8, 128), f32),
        in_specs=[hbm] * 5,
        out_specs=pl.BlockSpec(memory_space=pltpu.VMEM),
        scratch_shapes=[pltpu.VMEM(*a) for a in vmem]
        + [
            pltpu.SMEM((4,), f32),
            pltpu.SemaphoreType.DMA((3,)),
            pltpu.SemaphoreType.DMA((10,)),
            pltpu.SemaphoreType.DMA((10,)),
            pltpu.SemaphoreType.DMA((ITERS, 8)),
            pltpu.SemaphoreType.DMA((ITERS, 8)),
            pltpu.SemaphoreType.REGULAR((2,)),
        ],
        compiler_params=pltpu.CompilerParams(
            collective_id=0, has_side_effects=True, vmem_limit_bytes=32 * 2**20
        ),
        name="descent",
    )(
        *(
            pltpu.with_memory_space_constraint(v, pltpu.HBM)
            for v in (
                path.reshape(G, 4, 4, 8, 128),
                start_image.reshape(4, 4, 8, 128),
                end_image.reshape(4, 4, 8, 128),
                labels.reshape(4, 4, 8, 128),
                mob_table,
            )
        )
    )
    return result.reshape(path.shape)


def solution(mesh):
    field = P(None, "gy", None)
    return jax.shard_map(
        per_device,
        mesh=mesh,
        in_specs=(P("img", None, "gy", None), field, field, field, P()),
        out_specs=P("img", None, "gy", None),
        check_vma=False,
    )
```

time: 51.7 us -> 48.3 us (0.934)
  Pallas kernels: 50.9 us -> 47.5 us
    pallas_call x1, Pallas kernels: 50.9 us -> 47.5 us  [per_device(): pl.pallas_call(kernel, out_shape=jax.ShapeDtypeStruct((G, 4, 4, 8, 128),...]
where the time goes in v3:
time: 48.3 us; the launch traced here: 48.2 us
  Pallas kernels  47.5 us (98%)
  local copies, waits for them, and re-layouts  0.71 us (1%)
    pallas_call x1, Pallas kernels, per_device(): pl.pallas_call(kernel, out_shape=jax.ShapeDtypeStruct((G, 4, 4, 8, 128),...  47.5 us

profile of v3, /device:TPU:1, one launch (start us, length us, event | category | flops | bytes accessed | tf_op | source)
XLA Modules:
  0.0 48.2 jit_solution(14936456629043801886)
XLA Ops:
  0.0 47.5 %descent.1 = f32[4,4,4,8,128]{4,3,2,1,0:T(8,128)S(1)} custom-call(f32[4,4,4,8,128]{4,3,2,1,0:T(8,128)} %bitcast.6, f32[4,4,8,128]{3,2,1,0:T(8,128)} %bitcast.7, f32[4,4,8,128]{3,2,1,0:T(8,128)} %bitcast.8, s32[4,4,8,128]{3,2,1,0:T(8,128)} %bitcast.9, f32[4]{0:T(128)} %levels.1), custom_call_target="tpu_custom_call" | custom-call | tf_op jit(solution)/shard_map/descent/pallas_call | solution.py:380
  47.5 0.7 %copy.7 = f32[4,4,32,128]{3,2,1,0:T(8,128)} copy(f32[4,4,32,128]{3,2,1,0:T(8,128)S(1)} %bitcast.5) | data formatting | bytes 524288

commit v4 on v3

--- a/solution.py
+++ b/solution.py
@@ -170,10 +170,11 @@
         if i:
             mres[i, x] = mobb[x] * r
 
-    def quarter(i, x):
-        p = state[i, x]
+    def quarter(i, x, tiles):
+        p = state[i, x, pl.ds(0, tiles)]
         m, total = six(mres, i, x, sub)
-        return 0.5 * (res[i - 1, x] - res[i, x]) + ((0.125 + 0.75 * p * p) * m - 0.0625 * total)
+        moved = res[i - 1, x, pl.ds(0, tiles)] - res[i, x, pl.ds(0, tiles)]
+        return 0.5 * moved + ((0.125 + 0.75 * p * p) * m[:tiles] - 0.0625 * total[:tiles])
 
     cells = n_img * G * 4 * 32 * NX * 128
     zero = jnp.zeros((8, 128), jnp.float32)
@@ -209,7 +210,7 @@
         squares = jnp.zeros((4, 8, 128), jnp.float32)
         for turn in (2, 3, 1, 0):
             x = (k // 4 + turn) % 4
-            h1, h2, h3, h4 = (quarter(i, x) for i in range(1, G + 1))
+            h1, h2, h3, h4 = (quarter(i, x, 5 if it < ITERS - 1 else 4) for i in range(1, G + 1))
             v2 = -h1
             v3 = 2.0 * v2 - h2
             v4 = 2.0 * v3 - v2 - h3
@@ -226,7 +227,11 @@
                 if turn or t:
                     other = 4 * x + (k + t) % 4
                     send(s1.at[it, other, pl.ds(0, 2)], r1.at[it, k, pl.ds(0, 2)], it, 0, z * NK + other, gy)
-            ubuf[2, x], ubuf[3, x], ubuf[4, x], ubuf[5, x] = v2, v3, v4, 2.0 * v4 - v3 - h4
+            if it < ITERS - 1:
+                ubuf[2, x], ubuf[3, x], ubuf[4, x], ubuf[5, x] = v2, v3, v4, 2.0 * v4 - v3 - h4
+            else:
+                for n, w in enumerate((v2, v3, v4)):
+                    ubuf[2 + n, x, pl.ds(0, 4)] = w
             squares = squares + (v2 * v2 + v3 * v3 + v4 * v4)[:4]
         for m in PLANE:
             other = member(*m)
@@ -288,9 +293,6 @@
                     other = member(*m)
                     send(s3.at[it, other], r3h.at[slot], it, 7, z * NK + other, jnp.where(low_end, below, above))
 
-        for m in PLANE:
-            other = member(*m)
-            send(s3.at[it, other], r3.at[it, k], it, 6, z * NK + other, gy)
         r3[it, k] = s3[it, k]
 
         bytes_of(r2.at[it, pl.ds(0, NZ - 1), pl.ds(2, 3)], rcv.at[it, 3])
@@ -305,6 +307,9 @@
         for n, (*m, dx) in enumerate(NEAR):
             send(sa.at[it], ra.at[it, n], it, 5, z * NK + member(*m), (gy + dx) % NX)
 
+        for m in PLANE:
+            other = member(*m)
+            send(s3.at[it, other], r3.at[it, k], it, 6, z * NK + other, gy)
         bytes_of(r3.at[it, pl.ds(0, NK - 1)], rcv.at[it, 6])
 
         begin, slope = (r3[it, :, n].reshape(4, 4, 8, 128) for n in range(2))
@@ -334,11 +339,11 @@
                 ubuf[i] = u
 
         bytes_of(ra.at[it], rcv.at[it, 5])
-        total = sa[it]
-        for n in range(len(NEAR)):
-            total = total + ra[it, n]
-        mean = jnp.maximum(jnp.sum(total, 1, keepdims=True), 0.0) * (1.0 / cells)
-        scale = step_length / jnp.sqrt(mean + 1e-06)
+        rows = [sa[it]] + [ra[it, n] for n in range(len(NEAR))]
+        while len(rows) > 1:
+            rows = [a + b for a, b in zip(rows[::2], rows[1::2])]
+        mean = jnp.maximum(jnp.sum(rows[0], 1, keepdims=True), 0.0) * (1.0 / cells)
+        scale = step_length * lax.rsqrt(mean + 1e-06)
         if it == ITERS - 1:
             for i in range(1, G + 1):
                 out[i - 1] = state[i, :, pl.ds(0, 4)] - scale * ubuf[i, :, pl.ds(0, 4)]

time: 48.3 us -> 47.8 us (0.990)
  Pallas kernels: 47.5 us -> 47 us
    pallas_call x1, Pallas kernels: 47.5 us -> 47 us  [per_device(): pl.pallas_call(kernel, out_shape=jax.ShapeDtypeStruct((G, 4, 4, 8, 128),...]
where the time goes in v4:
time: 47.8 us; the launch traced here: 47.7 us
  Pallas kernels  47 us (98%)
  local copies, waits for them, and re-layouts  0.71 us (1%)
    pallas_call x1, Pallas kernels, per_device(): pl.pallas_call(kernel, out_shape=jax.ShapeDtypeStruct((G, 4, 4, 8, 128),...  47 us

profile of v4, /device:TPU:1, one launch (start us, length us, event | category | flops | bytes accessed | tf_op | source)
XLA Modules:
  0.0 47.7 jit_solution(5667701452015915858)
XLA Ops:
  0.0 47.0 %descent.1 = f32[4,4,4,8,128]{4,3,2,1,0:T(8,128)S(1)} custom-call(f32[4,4,4,8,128]{4,3,2,1,0:T(8,128)} %bitcast.6, f32[4,4,8,128]{3,2,1,0:T(8,128)} %bitcast.7, f32[4,4,8,128]{3,2,1,0:T(8,128)} %bitcast.8, s32[4,4,8,128]{3,2,1,0:T(8,128)} %bitcast.9, f32[4]{0:T(128)} %levels.1), custom_call_target="tpu_custom_call" | custom-call | tf_op jit(solution)/shard_map/descent/pallas_call | solution.py:385
  47.0 0.7 %copy.7 = f32[4,4,32,128]{3,2,1,0:T(8,128)} copy(f32[4,4,32,128]{3,2,1,0:T(8,128)S(1)} %bitcast.5) | data formatting | bytes 524288

commit v5 on v4

--- a/solution.py
+++ b/solution.py
@@ -39,7 +39,7 @@
 
 def kernel(
     path, start, end, labels, levels, out,
-    own, lab, edge, nxt, prv, labx, state, ubuf, mobb, res, mres,
+    own, lab, edge, nxt, prv, labx, state, ubuf, mobb, res, mres, sixp, sixu,
     s1, r1, ef, s2, r2, ud, s3, r3, r3h, sa, ra,
     table, loc, init_s, init_r, snd, rcv, relay,
 ):
@@ -160,8 +160,12 @@
     def bytes_of(ref, sem):
         pltpu.make_async_copy(ref, ref, sem).wait()
 
-    def force(i, x):
-        p, total = six(state, i, x, sub)
+    def force(i, x, it, scale):
+        if it == 0:
+            p, total = six(state, i, x, sub)
+            sixp[i, x] = total
+        else:
+            p, total = state[i, x], sixp[i, x] - scale * sixu[i, x]
         return p, mobb[x] * (stiffness * total - p * (0.5 + p * p))
 
     def keep(i, x, p, f):
@@ -178,6 +182,7 @@
 
     cells = n_img * G * 4 * 32 * NX * 128
     zero = jnp.zeros((8, 128), jnp.float32)
+    scale = None
     for it in range(ITERS):
         if it == 0:
             arrived((6, 7))
@@ -191,14 +196,14 @@
                 fill(i)
         for i in range(1, G):
             for x in range(4):
-                keep(i, x, *force(i, x))
+                keep(i, x, *force(i, x, it, scale))
         for x in range(4):
-            res[G, x] = force(G, x)[1]
+            res[G, x] = force(G, x, it, scale)[1]
         if it == 0:
             arrived((1, 2, 0))
             fill(0)
         for x in range(4):
-            keep(0, x, *force(0, x))
+            keep(0, x, *force(0, x, it, scale))
         if it == 0:
             arrived((4, 5, 3))
             fill(G + 1)
@@ -336,7 +341,10 @@
                     u = u + ubuf[i]
                 if i == G + 1:
                     u = u * last
-                ubuf[i] = u
+                ubuf[i] = jnp.concatenate([u[:, :4], u[:, 4:] * inside], 1)
+            for i in range(G + 1):
+                for x in range(4):
+                    sixu[i, x] = six(ubuf, i, x, sub)[1]
 
         bytes_of(ra.at[it], rcv.at[it, 5])
         rows = [sa[it]] + [ra[it, n] for n in range(len(NEAR))]
@@ -348,10 +356,8 @@
             for i in range(1, G + 1):
                 out[i - 1] = state[i, :, pl.ds(0, 4)] - scale * ubuf[i, :, pl.ds(0, 4)]
         else:
-            step = scale * inside
             for i in range(G + 2):
-                state[i, :, pl.ds(0, 4)] = state[i, :, pl.ds(0, 4)] - scale * ubuf[i, :, pl.ds(0, 4)]
-                state[i, :, pl.ds(4, 1)] = state[i, :, pl.ds(4, 1)] - step * ubuf[i, :, pl.ds(4, 1)]
+                state[i] = state[i] - scale * ubuf[i]
 
     for copy in halo:
         copy.wait_send()
@@ -376,7 +382,7 @@
         ((G, 4, 4, 8, 128), f32), ((4, 4, 8, 128), jnp.int32), ((2, 4, 4, 8, 128), f32),
         ((G + 2, 4, 8, 128), f32), ((G + 2, 4, 8, 128), f32), ((2, 4, 8, 128), jnp.int32),
         ((G + 2, 4, 5, 8, 128), f32), ((G + 2, 4, 5, 8, 128), f32), ((4, 5, 8, 128), f32),
-        ((G + 1, 4, 5, 8, 128), f32), ((G + 1, 4, 5, 8, 128), f32),
+        *[((G + 1, 4, 5, 8, 128), f32)] * 4,
         ((ITERS, NK, 4, 8, 128), f32), ((ITERS, NK, 4, 8, 128), f32), ((NK, 2, 8, 128), f32),
         ((ITERS, 5, 8, 128), f32), ((ITERS, NZ, 5, 8, 128), f32), ((NZ, 2, 8, 128), f32),
         ((ITERS, NK, 2, 8, 128), f32), ((ITERS, NK, 2, 8, 128), f32), ((8, 2, 8, 128), f32),

time: 47.8 us -> 47.9 us (level)
  no operation moved by 1% of the time
where the time goes in v5:
time: 47.9 us; the launch traced here: 47.8 us
  Pallas kernels  47.1 us (98%)
  local copies, waits for them, and re-layouts  0.71 us (1%)
    pallas_call x1, Pallas kernels, per_device(): pl.pallas_call(kernel, out_shape=jax.ShapeDtypeStruct((G, 4, 4, 8, 128),...  47.1 us

profile of v5, /device:TPU:1, one launch (start us, length us, event | category | flops | bytes accessed | tf_op | source)
XLA Modules:
  0.0 47.8 jit_solution(14840086149047557831)
XLA Ops:
  0.0 47.1 %descent.1 = f32[4,4,4,8,128]{4,3,2,1,0:T(8,128)S(1)} custom-call(f32[4,4,4,8,128]{4,3,2,1,0:T(8,128)} %bitcast.6, f32[4,4,8,128]{3,2,1,0:T(8,128)} %bitcast.7, f32[4,4,8,128]{3,2,1,0:T(8,128)} %bitcast.8, s32[4,4,8,128]{3,2,1,0:T(8,128)} %bitcast.9, f32[4]{0:T(128)} %levels.1), custom_call_target="tpu_custom_call" | custom-call | tf_op jit(solution)/shard_map/descent/pallas_call | solution.py:391
  47.1 0.7 %copy.7 = f32[4,4,32,128]{3,2,1,0:T(8,128)} copy(f32[4,4,32,128]{3,2,1,0:T(8,128)S(1)} %bitcast.5) | data formatting | bytes 524288

commit v6 on v4

--- a/solution.py
+++ b/solution.py
@@ -293,6 +293,10 @@
                     other = member(*m)
                     send(s3.at[it, other], r3h.at[slot], it, 7, z * NK + other, jnp.where(low_end, below, above))
 
+        if it == ITERS - 1:
+            for m in PLANE:
+                other = member(*m)
+                send(s3.at[it, other], r3.at[it, k], it, 6, z * NK + other, gy)
         r3[it, k] = s3[it, k]
 
         bytes_of(r2.at[it, pl.ds(0, NZ - 1), pl.ds(2, 3)], rcv.at[it, 3])
@@ -307,9 +311,10 @@
         for n, (*m, dx) in enumerate(NEAR):
             send(sa.at[it], ra.at[it, n], it, 5, z * NK + member(*m), (gy + dx) % NX)
 
-        for m in PLANE:
-            other = member(*m)
-            send(s3.at[it, other], r3.at[it, k], it, 6, z * NK + other, gy)
+        if it < ITERS - 1:
+            for m in PLANE:
+                other = member(*m)
+                send(s3.at[it, other], r3.at[it, k], it, 6, z * NK + other, gy)
         bytes_of(r3.at[it, pl.ds(0, NK - 1)], rcv.at[it, 6])
 
         begin, slope = (r3[it, :, n].reshape(4, 4, 8, 128) for n in range(2))

time: 47.8 us -> 47.8 us (level)
  no operation moved by 1% of the time
where the time goes in v6:
time: 47.8 us; the launch traced here: 47.7 us
  Pallas kernels  47 us (98%)
  local copies, waits for them, and re-layouts  0.71 us (1%)
    pallas_call x1, Pallas kernels, per_device(): pl.pallas_call(kernel, out_shape=jax.ShapeDtypeStruct((G, 4, 4, 8, 128),...  47 us

profile of v6, /device:TPU:1, one launch (start us, length us, event | category | flops | bytes accessed | tf_op | source)
XLA Modules:
  0.0 47.7 jit_solution(7332413306011242732)
XLA Ops:
  0.0 47.0 %descent.1 = f32[4,4,4,8,128]{4,3,2,1,0:T(8,128)S(1)} custom-call(f32[4,4,4,8,128]{4,3,2,1,0:T(8,128)} %bitcast.6, f32[4,4,8,128]{3,2,1,0:T(8,128)} %bitcast.7, f32[4,4,8,128]{3,2,1,0:T(8,128)} %bitcast.8, s32[4,4,8,128]{3,2,1,0:T(8,128)} %bitcast.9, f32[4]{0:T(128)} %levels.1), custom_call_target="tpu_custom_call" | custom-call | tf_op jit(solution)/shard_map/descent/pallas_call | solution.py:390
  47.0 0.7 %copy.7 = f32[4,4,32,128]{3,2,1,0:T(8,128)} copy(f32[4,4,32,128]{3,2,1,0:T(8,128)S(1)} %bitcast.5) | data formatting | bytes 524288
